TPU v7x, 32 devices: a whole 2x2x4 slice. The times are simulated.
32 devices in a mesh: obs: 8 (over y, x, core), rows: 4 (over z).
Axes of the slice: x: 2, y: 2, z: 4, core: 2. Of those that a mesh axis runs over, the one named last changes fastest.
Arguments:
- state: float32 [8192, 256], P(('obs', 'rows')), may hold values from -6 to 6
- foot_tiles: int32 [192, 4], P('obs'), may hold values from 0 to 3
- foot_weight: float32 [192, 4, 256], P('obs'), may hold values from -0.25 to 0.25
- azimuth: float32 [768], P('obs'), may hold values from -3.140625 to 3.140625
- obs_value: float32 [768], replicated, may hold values from 0.5 to 2.5
- obs_var: float32 [768], replicated, may hold values from 0.3 to 3
- tile_bin: int32 [32, 768], P(('obs', 'rows')), may hold values from 0 to 14
- obs_bin: int32 [768, 768], P('obs'), may hold values from 0 to 14
- order: int32 [768], replicated, may hold values from 0 to 767, as said below
Outputs:
- analysis: float32 [8192, 256], P(('obs', 'rows'))
Inputs may be any that keep to these rules, and one draw needn't show every extreme that they name: foot_tiles numbers a tile among the 4 tiles of the footprint's own observation group. `order`: a permutation of the observables; each aligned block of 128 entries is one batch, and every batch holds equally many observables of each observation group (the 96 observables of group g are g * 96 to g * 96 + 95).
All inputs are finite; a program needn't handle non-finite values.
Results may differ from a plain program's by a relative error of at most 0.0003.
Values sent between devices are 32-bit elements; how exact they have to be, the bound alone decides.
A program may use at most 64 MiB of HBM per device.

v0:
```python
import functools

import jax
import jax.numpy as jnp
from jax import lax
from jax.experimental import pallas as pl
from jax.experimental.pallas import tpu as pltpu
from jax.sharding import PartitionSpec as P

MEMBERS = 256
BATCH = 128
TILE = 256
RADIUS = 8
SUB = 8
STAGES = 8
F32 = jnp.float32
BF16 = jnp.bfloat16


HIGH = lax.Precision.HIGHEST
MESH = pl.DeviceIdType.MESH
VMEM = pl.BlockSpec(memory_space=pltpu.VMEM)


def model_function(east_wind, north_wind, cosines, sines):
    speed = jnp.sqrt(east_wind * east_wind + north_wind * north_wind + 1.0)
    cosine = (east_wind * cosines + north_wind * sines) / speed
    return jnp.exp(0.6 * jnp.log(speed)) * (0.7 + 0.4 * cosine + 0.6 * cosine * cosine)


def taper_weight(bins):
    scaled = 1.0 - bins.astype(F32) / RADIUS
    return jnp.where(bins < RADIUS, scaled * scaled, jnp.zeros_like(scaled))


def halves(value):
    high = value.astype(BF16)
    return high, (value - high.astype(F32)).astype(BF16)


def dot3(left, right, dims):
    (left_hi, left_lo), (right_hi, right_lo) = left, right
    (left_dim,), (right_dim,) = dims
    return lax.dot_general(
        jnp.concatenate([left_hi, left_lo, left_hi], left_dim),
        jnp.concatenate([right_hi, right_hi, right_lo], right_dim),
        (dims, ((), ())),
        preferred_element_type=F32,
    )


NN = ((1,), (0,))
NT = ((1,), (1,))
TN = ((0,), (0,))


def total(terms):
    while len(terms) > 1:
        terms = [a + b for a, b in zip(terms[::2], terms[1::2])]
    return terms[0]


def factor(panel, roots, upper, stage):
    blocks, half = BATCH // SUB, BATCH // 2
    lane = lax.broadcasted_iota(jnp.int32, (SUB, BATCH), 1)
    sub = lax.broadcasted_iota(jnp.int32, (SUB, BATCH), 0)
    left, right = pl.ds(0, BATCH), pl.ds(BATCH, BATCH)

    def across(value, column):
        lanes = jnp.full((SUB, BATCH), column, jnp.int32)
        return jnp.take_along_axis(value, lanes, axis=1, mode="promise_in_bounds")

    def down(value, row):
        return jnp.broadcast_to(value[row : row + 1, :], (SUB, BATCH))

    def rows(i):
        return pl.ds(SUB * i, SUB)

    for b in range(blocks):
        base = SUB * b
        end = blocks if base >= half else blocks // 2
        inside = jnp.logical_and(lane >= base, lane < base + SUB)
        start = panel[rows(b), left]
        given = panel[rows(b), right]
        root = roots[rows(b), :]
        cols = [across(start, base + k) for k in range(SUB)]
        for i in range(b + 1, end):
            value = panel[rows(i), left]
            for k in range(SUB):
                stage[i % STAGES, k] = across(value, base + k)
        solved = jnp.where(inside, (lane == sub + base).astype(F32), start)
        forward, scale, diagonal, steps = solved, None, None, []
        for k in range(0, SUB, 2):
            one, two = sub == k, sub == k + 1
            pair, below = jnp.logical_or(one, two), sub > k + 1
            u, v = cols[k], cols[k + 1]
            a, e, c = down(u, k), down(u, k + 1), down(v, k + 1)
            det = a * c - e * e
            inv_det_root, inv_root = lax.rsqrt(det), lax.rsqrt(a)
            inv = inv_det_root * inv_det_root
            p = jnp.where(one, -c, jnp.where(two, e, c * u - e * v))
            q = jnp.where(one, e, jnp.where(two, -a, a * v - e * u))
            for m in range(k + 2, SUB):
                cols[m] = jnp.where(pair, 0.0, cols[m]) - (p * down(u, m) + q * down(v, m)) * inv
            full_p, full_q = p * inv, q * inv
            solved = jnp.where(pair, 0.0, solved) - (full_p * down(solved, k) + full_q * down(solved, k + 1))
            ratio = e * (inv_root * inv_root)
            part_p = jnp.where(below, full_p, jnp.where(two, ratio, 0.0))
            part_q = jnp.where(below, full_q, 0.0)
            forward = forward - (part_p * down(forward, k) + part_q * down(forward, k + 1))
            second_scale = inv_det_root * (a * inv_root)
            diag_one, diag_two = a * inv_root, det * inv_det_root * inv_root
            if k == 0:
                scale, diagonal = jnp.where(one, inv_root, second_scale), jnp.where(one, diag_one, diag_two)
            else:
                scale = jnp.where(one, inv_root, jnp.where(two, second_scale, scale))
                diagonal = jnp.where(one, diag_one, jnp.where(two, diag_two, diagonal))
            steps.append((k, full_p, full_q, pair, u * inv_root, (v - u * ratio) * second_scale, one, two, below))
        forward = forward * scale
        lower = jnp.where(lane <= sub + base, forward, 0.0)
        panel[rows(b), left] = lower
        if base < half:
            upper[rows(b), :] = jnp.where(lane < half, lower, forward)
        gain = 1.0 / (diagonal + root)
        own = given
        for k, _, _, _, low, next_low, one, two, below in steps:
            first = down(own, k) * down(gain, k)
            second = (down(own, k + 1) - down(low, k + 1) * first) * down(gain, k + 1)
            rest = own - (low * first + next_low * second)
            own = jnp.where(below, rest, jnp.where(one, first, jnp.where(two, second, own)))
        panel[rows(b), right] = own
        if b + 1 < end:
            spread = given - root * own
            for k, full_p, full_q, pair, *_ in steps:
                spread = jnp.where(pair, 0.0, spread) - (full_p * down(spread, k) + full_q * down(spread, k + 1))
            for i in range(b + 1, end):
                columns = [stage[i % STAGES, k] for k in range(SUB)]
                value = jnp.where(inside, 0.0, panel[rows(i), left])
                panel[rows(i), left] = value - total([columns[k] * down(solved, k) for k in range(SUB)])
                panel[rows(i), right] = panel[rows(i), right] - total([columns[k] * down(spread, k) for k in range(SUB)])
        elif end < blocks:
            far = pl.ds(half, half)
            outer = halves(upper[...])
            wide = lax.broadcasted_iota(jnp.int32, (half, BATCH), 1)
            change = dot3(outer, outer, TN)[half:, :]
            panel[far, left] = jnp.where(wide < half, 0.0, panel[far, left]) - change
            change = dot3(outer, halves(panel[:half, right]), TN)[half:, :]
            panel[far, right] = panel[far, right] - change


def filter_kernel(
    group_size, state_ref, obs_ref, taper_ref, tile_ref, given_ref, order_ref, order_row_ref, out_ref, held, weights, picked_given,
    panel, roots, upper, stage,
):
    nobs = obs_ref.shape[0]
    batches = nobs // BATCH
    tiles_dev = tile_ref.shape[0]
    index = lax.broadcasted_iota(jnp.int32, (BATCH, nobs), 1)
    dot = functools.partial(jnp.dot, preferred_element_type=F32)

    lane = lax.broadcasted_iota(jnp.int32, (BATCH, BATCH), 1)
    before = lane < lax.broadcasted_iota(jnp.int32, (BATCH, BATCH), 0)

    def pick(select, value):
        high, rest = halves(value)
        low = (value - high.astype(F32) - rest.astype(F32)).astype(BF16)
        return dot(select, high) + (dot(select, rest) + dot(select, low))

    def arrange(num, carry):
        rows = pl.ds(pl.multiple_of(num * BATCH, BATCH), BATCH)
        wanted = order_ref[rows, :]
        select = (wanted == index).astype(F32).astype(BF16)
        picked_given[rows, :] = pick(select, given_ref[...])
        group = wanted // group_size
        same = jnp.logical_and(before, group == order_row_ref[:, rows] // group_size)
        earlier = jnp.sum(same.astype(F32), axis=1, keepdims=True).astype(jnp.int32)
        place = group * (group_size // batches) + earlier
        select = (place == lane).astype(F32).astype(BF16)
        held[rows, :] = pick(select, obs_ref[rows, :])
        weights[rows, :] = dot(select, taper_ref[rows, :].astype(BF16))
        return carry

    lax.fori_loop(0, batches, arrange, 0)
    out_ref[...] = state_ref[...]
    eye = lax.broadcasted_iota(jnp.int32, (BATCH, BATCH), 0) == lax.broadcasted_iota(
        jnp.int32, (BATCH, BATCH), 1
    )

    def batch_step(num, carry):
        rows = pl.ds(pl.multiple_of(num * BATCH, BATCH), BATCH)
        batch_obs = held[rows, :]
        row_mean = jnp.mean(batch_obs, axis=1, keepdims=True)
        perturb = batch_obs - row_mean
        given = picked_given[rows, :]
        innov = given[:, 0:1] - row_mean
        variance = given[:, 1:2]
        roots[...] = jnp.broadcast_to(jnp.sqrt(variance), (BATCH, BATCH))
        split = halves(perturb)
        scaled = halves(perturb * (1.0 / (MEMBERS - 1)))
        panel[:, :BATCH] = dot3(split, scaled, NT) + jnp.where(eye, variance, 0.0)
        panel[:, BATCH:] = eye.astype(F32)
        factor(panel, roots, upper, stage)
        first = halves(panel[:, :BATCH])
        second = panel[:, BATCH:]
        middle = dot3(first, halves(jnp.broadcast_to(innov, (BATCH, MEMBERS))), NN) - dot3(
            halves(second), split, NN
        )
        change = halves(dot3(first, halves(middle), TN))

        def update(ref, place, weight):
            value = ref[place, :]
            product = dot3(halves(value), scaled, NT) * weight
            ref[place, :] = value + dot3(halves(product), change, NN)

        def update_obs(other, inner):
            place = pl.ds(pl.multiple_of(other * BATCH, BATCH), BATCH)
            update(held, place, weights[place, rows])
            return inner

        lax.fori_loop(num + 1, batches, update_obs, 0)
        for tile in range(tiles_dev):
            update(out_ref, pl.ds(tile * TILE, TILE), tile_ref[tile : tile + 1, rows])
        return carry

    lax.fori_loop(0, batches, batch_step, 0)


def filter_all(state, every_obs, taper, tile_taper, given, order, group_size):
    nobs = every_obs.shape[0]
    return pl.pallas_call(
        functools.partial(filter_kernel, group_size),
        out_shape=jax.ShapeDtypeStruct(state.shape, F32),
        in_specs=[VMEM] * 7,
        out_specs=VMEM,
        scratch_shapes=[
            pltpu.VMEM((nobs, MEMBERS), F32),
            pltpu.VMEM((nobs, nobs), F32),
            pltpu.VMEM((nobs, given.shape[1]), F32),
            pltpu.VMEM((BATCH, 2 * BATCH), F32),
            pltpu.VMEM((BATCH, BATCH), F32),
            pltpu.VMEM((BATCH // 2, BATCH), F32),
            pltpu.VMEM((STAGES, SUB, SUB, BATCH), F32),
        ],
        compiler_params=pltpu.CompilerParams(vmem_limit_bytes=48 * 1024 * 1024),
    )(state, every_obs, taper, tile_taper, given, order[:, None], order[None, :])


def exchange_kernel(
    groups, layers, state_ref, tiles_ref, weight_ref, cos_ref, sin_ref, order_ref, bins_ref, tile_bin_ref,
    obs_out, taper_out, tile_out, own_sums, sums, own_obs, own_taper,
    sum_send, sum_recv, obs_send, obs_recv, taper_send, taper_recv,
):
    me, layer = lax.axis_index("obs"), lax.axis_index("rows")
    feet, batches, per = tiles_ref.shape[0], own_obs.shape[0], own_obs.shape[1]
    count, nobs = bins_ref.shape
    tiles_dev, half = tile_bin_ref.shape[0], TILE // 2
    barrier = pltpu.get_barrier_semaphore()
    for k in range(1, groups):
        pl.semaphore_signal(barrier, inc=1, device_id={"obs": lax.rem(me + k, groups)}, device_id_type=MESH)
    for k in range(1, layers):
        pl.semaphore_signal(barrier, inc=1, device_id={"rows": lax.rem(layer + k, layers)}, device_id_type=MESH)

    partial = [jnp.zeros((feet, MEMBERS), F32) for _ in range(2)]
    for tile in range(tiles_dev):
        number = layer * tiles_dev + tile
        factor = jnp.zeros((feet, TILE), F32)
        for t in range(tiles_ref.shape[1]):
            factor = factor + jnp.where(tiles_ref[:, t : t + 1] == number, weight_ref[:, t, :], 0.0)
        for h in range(2):
            partial[h] = partial[h] + jnp.dot(
                factor[:, h * half : (h + 1) * half],
                state_ref[pl.ds(tile * TILE + h * half, half), :],
                precision=HIGH,
                preferred_element_type=F32,
            )
    for h in range(2):
        own_sums[h] = partial[h]
    pl.semaphore_wait(barrier, groups + layers - 2)

    sum_copies = []
    for k in range(1, layers):
        copy = pltpu.make_async_remote_copy(
            own_sums, sums.at[k], sum_send.at[k], sum_recv.at[k],
            device_id={"rows": lax.rem(layer + k, layers)}, device_id_type=MESH,
        )
        copy.start()
        sum_copies.append(copy)

    order = order_ref[...]
    base = me * count
    steps = lax.broadcasted_iota(jnp.int32, (count, nobs), 1).astype(F32)
    member = jnp.logical_and(order >= base, order < base + count).astype(F32)
    local = lax.broadcasted_iota(jnp.int32, (count, 1), 0)
    column = lax.broadcasted_iota(jnp.int32, (count, count), 1)

    def ranks(ids):
        at = jnp.sum(jnp.where(order == base + ids, steps, 0.0), axis=1, keepdims=True)
        rank = jnp.sum(jnp.where(steps < at, member, 0.0), axis=1, keepdims=True)
        return (rank.astype(jnp.int32) == column).astype(F32)

    sorter = (lax.broadcasted_iota(jnp.int32, (nobs, nobs), 0) == order).astype(F32).astype(BF16)
    ordered = jnp.dot(taper_weight(bins_ref[...]).astype(BF16), sorter, preferred_element_type=F32)
    ordered = lax.dot_general(
        ranks(local).astype(BF16), ordered.astype(BF16), (TN, ((), ())), preferred_element_type=F32
    )
    for b in range(batches):
        own_taper[b] = ordered[b * per : (b + 1) * per, :]
        taper_out[b, me] = ordered[b * per : (b + 1) * per, :]
    cuts = [(b, 1) for b in range(1, batches)]
    taper_copies = []
    for k in range(1, groups):
        for c, (first, length) in enumerate(cuts):
            wide = pl.ds(0, (first + length - 1) * BATCH)
            copy = pltpu.make_async_remote_copy(
                own_taper.at[pl.ds(first, length), :, wide],
                taper_out.at[pl.ds(first, length), me, :, wide],
                taper_send.at[k, c], taper_recv.at[k, c],
                device_id={"obs": lax.rem(me + k, groups)}, device_id_type=MESH,
            )
            copy.start()
            taper_copies.append(copy)

    tile_out[...] = jnp.dot(taper_weight(tile_bin_ref[...]).astype(BF16), sorter, preferred_element_type=F32)
    chooser = ranks(local % feet * 4 + local // feet)
    for copy in sum_copies:
        copy.wait()
    winds = [own_sums[h] for h in range(2)]
    for k in range(1, layers):
        winds = [winds[h] + sums[k, h] for h in range(2)]
    observed = jnp.concatenate(
        [
            model_function(winds[0], winds[1], cos_ref[:, k : k + 1], sin_ref[:, k : k + 1])
            for k in range(cos_ref.shape[1])
        ],
        0,
    )
    observed = lax.dot_general(chooser, observed, (TN, ((), ())), precision=HIGH, preferred_element_type=F32)
    for b in range(batches):
        own_obs[b] = observed[b * per : (b + 1) * per, :]
        obs_out[b, me] = observed[b * per : (b + 1) * per, :]
    obs_copies = []
    for k in range(1, groups):
        copy = pltpu.make_async_remote_copy(
            own_obs, obs_out.at[:, me], obs_send.at[k], obs_recv.at[k],
            device_id={"obs": lax.rem(me + k, groups)}, device_id_type=MESH,
        )
        copy.start()
        obs_copies.append(copy)
    for copy in taper_copies + obs_copies:
        copy.wait()


def exchange(state, foot_tiles, foot_weight, cosines, sines, order_row, obs_bin, tile_bin):
    groups, layers = lax.axis_size("obs"), lax.axis_size("rows")
    count, nobs = obs_bin.shape
    batches, feet = nobs // BATCH, foot_tiles.shape[0]
    per = count // batches
    dma = pltpu.SemaphoreType.DMA
    return pl.pallas_call(
        functools.partial(exchange_kernel, groups, layers),
        out_shape=(
            jax.ShapeDtypeStruct((batches, groups, per, MEMBERS), F32),
            jax.ShapeDtypeStruct((batches, groups, per, nobs), F32),
            jax.ShapeDtypeStruct(tile_bin.shape, F32),
        ),
        in_specs=[VMEM] * 8,
        out_specs=(VMEM, VMEM, VMEM),
        scratch_shapes=[
            pltpu.VMEM((2, feet, MEMBERS), F32),
            pltpu.VMEM((layers, 2, feet, MEMBERS), F32),
            pltpu.VMEM((batches, per, MEMBERS), F32),
            pltpu.VMEM((batches, per, nobs), F32),
            dma((layers,)), dma((layers,)), dma((groups,)), dma((groups,)), dma((groups, batches)), dma((groups, batches)),
        ],
        compiler_params=pltpu.CompilerParams(
            collective_id=0, has_side_effects=True, vmem_limit_bytes=48 * 1024 * 1024
        ),
    )(state, foot_tiles, foot_weight, cosines, sines, order_row, obs_bin, tile_bin)


def shards(state, foot_tiles, foot_weight, azimuth, obs_value, obs_var, tile_bin, obs_bin, order):
    angles = azimuth.reshape(foot_tiles.shape[0], -1)
    every_obs, taper, tile_taper = exchange(
        state, foot_tiles, foot_weight, jnp.cos(angles), jnp.sin(angles), order[None, :], obs_bin, tile_bin
    )
    nobs = order.shape[0]
    given = jnp.stack([obs_value, obs_var], axis=1)
    return filter_all(
        state, every_obs.reshape(nobs, MEMBERS), taper.reshape(nobs, nobs), tile_taper, given, order, obs_bin.shape[0]
    )


def solution(mesh):
    return jax.shard_map(
        shards,
        mesh=mesh,
        in_specs=(
            P(("obs", "rows"), None),
            P("obs", None),
            P("obs", None, None),
            P("obs"),
            P(),
            P(),
            P(("obs", "rows"), None),
            P("obs", None),
            P(),
        ),
        out_specs=P(("obs", "rows"), None),
        check_vma=False,
    )
```

profile of v0, /device:TPU:0, one launch (start us, length us, event | category | flops | bytes accessed | tf_op | source)
XLA Modules:
  0.0 70.8 jit_solution(1665768279401089172)
XLA Ops:
  0.0 0.7 fusion
  0.7 0.7 broadcast_in_dim.7.order_ref.order_row_ref
  1.4 0.7 stack.9
  2.1 0.7 stack.10
  2.8 0.1 sin.6.sin_ref
  2.9 0.1 cos.6.cos_ref
  3.0 0.8 %copy.15.tiles_ref = s32[24,4]{1,0:T(8,128)S(1)} copy(s32[24,4]{0,1:T(4,128)} %param.10) | data formatting | bytes 768 | tf_op args[1]
  3.7 0.2 copy.16.given_ref
  3.9 0.8 %broadcast_in_dim.9.order_ref = s32[768,1]{1,0:T(8,128)S(1)} reshape(s32[768]{0:T(1024)} %param.17) | data formatting | bytes 6144 | tf_op jit(solution)/shard_map/broadcast_in_dim | solution.py:245
  4.8 0.0 copy-start
  4.8 0.9 %copy-done = f32[256,256]{1,0:T(8,128)S(1)} copy-done((f32[256,256]{1,0:T(8,128)S(1)}, f32[256,256]{1,0:T(8,128)}, u32[]{:S(2)}) %copy-start) | copy-done | bytes 262168
  5.7 0.0 copy-start.1
  5.7 1.0 %copy-done.1 = s32[96,768]{1,0:T(8,128)S(1)} copy-done((s32[96,768]{1,0:T(8,128)S(1)}, s32[96,768]{1,0:T(8,128)}, u32[]{:S(2)}) %copy-start.1) | copy-done | bytes 294936
  6.7 0.0 copy-start.2
  6.7 0.9 %copy-done.2 = f32[24,4,256]{2,1,0:T(4,128)S(1)} copy-done((f32[24,4,256]{2,1,0:T(4,128)S(1)}, f32[24,4,256]{2,1,0:T(4,128)}, u32[]{:S(2)}) %copy-start.2) | copy-done | bytes 98328
  7.6 0.0 copy-start.3
  7.6 0.7 copy-done.3
  8.3 26.8 %shard_map.91 = (f32[6,8,16,256]{3,2,1,0:T(8,128)S(1)}, f32[6,8,16,768]{3,2,1,0:T(8,128)S(1)}, f32[1,768]{1,0:T(1,128)S(1)}) custom-call(f32[256,256]{1,0:T(8,128)S(1)} %copy-done, s32[24,4]{1,0:T(8,128)S(1)} %copy.15.tiles_ref, f32[24,4,256]{2,1,0:T(4,128)S(1)} %copy-done.2, f32[24,4]{1,0:T(8,128)S(1)} %cos.6.cos_ref, f32[24,4]{1,0:T(8,128)S(1)} %sin.6.sin_ref, ...), custom_call_target="tpu_custom_call" | custom-call | tf_op jit(solution)/shard_map/pallas_call | solution.py:359
  35.1 35.7 %shard_map.92 = f32[256,256]{1,0:T(8,128)} custom-call(f32[256,256]{1,0:T(8,128)S(1)} %copy-done, f32[768,256]{1,0:T(8,128)S(1)} %bitcast.3, f32[768,768]{1,0:T(8,128)S(1)} %bitcast.2, f32[1,768]{1,0:T(1,128)S(1)} %get-tuple-element.10.tile_ref, f32[768,2]{1,0:T(8,128)S(1)} %copy.16.given_ref, s32[768,1]{1,0:T(8,128)S(1)} %broadcast_in_dim.9.order_ref, ...), custom_call_target="tpu_custom_call" | custom-call | tf_op jit(solution)/shard_map/pallas_call | solution.py:230
  (1 shorter events, 0.0 us)
Async XLA Ops:
  4.8 1.0 %copy-start = (f32[256,256]{1,0:T(8,128)S(1)}, f32[256,256]{1,0:T(8,128)}, u32[]{:S(2)}) copy-start(f32[256,256]{1,0:T(8,128)} %state_ref.3) | copy-start | bytes 786436
  5.7 1.0 %copy-start.1 = (s32[96,768]{1,0:T(8,128)S(1)}, s32[96,768]{1,0:T(8,128)}, u32[]{:S(2)}) copy-start(s32[96,768]{1,0:T(8,128)} %bins_ref.1) | copy-start | bytes 884740
  6.7 0.9 %copy-start.2 = (f32[24,4,256]{2,1,0:T(4,128)S(1)}, f32[24,4,256]{2,1,0:T(4,128)}, u32[]{:S(2)}) copy-start(f32[24,4,256]{2,1,0:T(4,128)} %weight_ref.1) | copy-start | bytes 294916
  7.6 0.7 copy-start.3
where the time goes:
time: 71.5 us; the launch traced here: 70.8 us
  Pallas kernels  62.5 us (87%)
  local copies, waits for them, and re-layouts  8.22 us (11%)
    pallas_call x1, Pallas kernels, filter_all(): pl.pallas_call(functools.partial(filter_kernel, group_size), out_shape=ja...  35.7 us
    pallas_call x1, Pallas kernels, exchange(): pl.pallas_call(functools.partial(exchange_kernel, groups, layers), out_sh...  26.8 us
    unnamed x9, local copies, waits for them, and re-layouts  4.25 us
    another operation x3, local copies, waits for them, and re-layouts, shards(): given = jnp.stack([obs_value, obs_var], axis=1)  1.56 us

commit v1 on v0

v1 whole, which is shorter than its diff:
```python
import functools

import jax
import jax.numpy as jnp
from jax import lax
from jax.experimental import pallas as pl
from jax.experimental.pallas import tpu as pltpu
from jax.sharding import PartitionSpec as P

MEMBERS = 256
BATCH = 128
TILE = 256
RADIUS = 8
SUB = 8
STAGES = 8
F32 = jnp.float32
BF16 = jnp.bfloat16


HIGH = lax.Precision.HIGHEST
MESH = pl.DeviceIdType.MESH
VMEM = pl.BlockSpec(memory_space=pltpu.VMEM)
ANY = pl.BlockSpec(memory_space=pl.ANY)


def model_function(east_wind, north_wind, cosines, sines):
    speed = jnp.sqrt(east_wind * east_wind + north_wind * north_wind + 1.0)
    cosine = (east_wind * cosines + north_wind * sines) / speed
    return jnp.exp(0.6 * jnp.log(speed)) * (0.7 + 0.4 * cosine + 0.6 * cosine * cosine)


def taper_weight(bins):
    scaled = 1.0 - bins.astype(F32) / RADIUS
    return jnp.where(bins < RADIUS, scaled * scaled, jnp.zeros_like(scaled))


def halves(value):
    high = value.astype(BF16)
    return high, (value - high.astype(F32)).astype(BF16)


def dot3(left, right, dims):
    (left_hi, left_lo), (right_hi, right_lo) = left, right
    (left_dim,), (right_dim,) = dims
    return lax.dot_general(
        jnp.concatenate([left_hi, left_lo, left_hi], left_dim),
        jnp.concatenate([right_hi, right_hi, right_lo], right_dim),
        (dims, ((), ())),
        preferred_element_type=F32,
    )


NN = ((1,), (0,))
NT = ((1,), (1,))
TN = ((0,), (0,))


def total(terms):
    while len(terms) > 1:
        terms = [a + b for a, b in zip(terms[::2], terms[1::2])]
    return terms[0]


def factor(panel, roots, upper, stage):
    blocks, half = BATCH // SUB, BATCH // 2
    lane = lax.broadcasted_iota(jnp.int32, (SUB, BATCH), 1)
    sub = lax.broadcasted_iota(jnp.int32, (SUB, BATCH), 0)
    left, right = pl.ds(0, BATCH), pl.ds(BATCH, BATCH)

    def across(value, column):
        lanes = jnp.full((SUB, BATCH), column, jnp.int32)
        return jnp.take_along_axis(value, lanes, axis=1, mode="promise_in_bounds")

    def down(value, row):
        return jnp.broadcast_to(value[row : row + 1, :], (SUB, BATCH))

    def rows(i):
        return pl.ds(SUB * i, SUB)

    for b in range(blocks):
        base = SUB * b
        end = blocks if base >= half else blocks // 2
        inside = jnp.logical_and(lane >= base, lane < base + SUB)
        start = panel[rows(b), left]
        given = panel[rows(b), right]
        root = roots[rows(b), :]
        cols = [across(start, base + k) for k in range(SUB)]
        for i in range(b + 1, end):
            value = panel[rows(i), left]
            for k in range(SUB):
                stage[i % STAGES, k] = across(value, base + k)
        solved = jnp.where(inside, (lane == sub + base).astype(F32), start)
        forward, scale, diagonal, steps = solved, None, None, []
        for k in range(0, SUB, 2):
            one, two = sub == k, sub == k + 1
            pair, below = jnp.logical_or(one, two), sub > k + 1
            u, v = cols[k], cols[k + 1]
            a, e, c = down(u, k), down(u, k + 1), down(v, k + 1)
            det = a * c - e * e
            inv_det_root, inv_root = lax.rsqrt(det), lax.rsqrt(a)
            inv = inv_det_root * inv_det_root
            p = jnp.where(one, -c, jnp.where(two, e, c * u - e * v))
            q = jnp.where(one, e, jnp.where(two, -a, a * v - e * u))
            for m in range(k + 2, SUB):
                cols[m] = jnp.where(pair, 0.0, cols[m]) - (p * down(u, m) + q * down(v, m)) * inv
            full_p, full_q = p * inv, q * inv
            solved = jnp.where(pair, 0.0, solved) - (full_p * down(solved, k) + full_q * down(solved, k + 1))
            ratio = e * (inv_root * inv_root)
            part_p = jnp.where(below, full_p, jnp.where(two, ratio, 0.0))
            part_q = jnp.where(below, full_q, 0.0)
            forward = forward - (part_p * down(forward, k) + part_q * down(forward, k + 1))
            second_scale = inv_det_root * (a * inv_root)
            diag_one, diag_two = a * inv_root, det * inv_det_root * inv_root
            if k == 0:
                scale, diagonal = jnp.where(one, inv_root, second_scale), jnp.where(one, diag_one, diag_two)
            else:
                scale = jnp.where(one, inv_root, jnp.where(two, second_scale, scale))
                diagonal = jnp.where(one, diag_one, jnp.where(two, diag_two, diagonal))
            steps.append((k, full_p, full_q, pair, u * inv_root, (v - u * ratio) * second_scale, one, two, below))
        forward = forward * scale
        lower = jnp.where(lane <= sub + base, forward, 0.0)
        panel[rows(b), left] = lower
        if base < half:
            upper[rows(b), :] = jnp.where(lane < half, lower, forward)
        gain = 1.0 / (diagonal + root)
        own = given
        for k, _, _, _, low, next_low, one, two, below in steps:
            first = down(own, k) * down(gain, k)
            second = (down(own, k + 1) - down(low, k + 1) * first) * down(gain, k + 1)
            rest = own - (low * first + next_low * second)
            own = jnp.where(below, rest, jnp.where(one, first, jnp.where(two, second, own)))
        panel[rows(b), right] = own
        if b + 1 < end:
            spread = given - root * own
            for k, full_p, full_q, pair, *_ in steps:
                spread = jnp.where(pair, 0.0, spread) - (full_p * down(spread, k) + full_q * down(spread, k + 1))
            for i in range(b + 1, end):
                columns = [stage[i % STAGES, k] for k in range(SUB)]
                value = jnp.where(inside, 0.0, panel[rows(i), left])
                panel[rows(i), left] = value - total([columns[k] * down(solved, k) for k in range(SUB)])
                panel[rows(i), right] = panel[rows(i), right] - total([columns[k] * down(spread, k) for k in range(SUB)])
        elif end < blocks:
            far = pl.ds(half, half)
            outer = halves(upper[...])
            wide = lax.broadcasted_iota(jnp.int32, (half, BATCH), 1)
            change = dot3(outer, outer, TN)[half:, :]
            panel[far, left] = jnp.where(wide < half, 0.0, panel[far, left]) - change
            change = dot3(outer, halves(panel[:half, right]), TN)[half:, :]
            panel[far, right] = panel[far, right] - change


def pick(select, value):
    high, rest = halves(value)
    low = (value - high.astype(F32) - rest.astype(F32)).astype(BF16)
    dot = functools.partial(jnp.dot, preferred_element_type=F32)
    return dot(select, high) + (dot(select, rest) + dot(select, low))


def lookup(pieces, index):
    inner, outer = index % BATCH, index // BATCH
    found = jnp.zeros(index.shape, pieces[0].dtype)
    for q, piece in enumerate(pieces):
        piece = jnp.broadcast_to(piece, index.shape)
        piece = jnp.take_along_axis(piece, inner, axis=1, mode="promise_in_bounds")
        found = jnp.where(outer == q, piece, found)
    return found


def iota(shape, dim):
    return lax.broadcasted_iota(jnp.int32, shape, dim)


def column_of(row):
    size = row.shape[1]
    eye = iota((size, size), 0) == iota((size, size), 1)
    return jnp.sum(jnp.where(eye, row, jnp.zeros_like(row)), axis=1, keepdims=True)


def filter_kernel(
    groups, layers, state_hbm, tiles_hbm, weight_hbm, azimuth_hbm, value_hbm, var_hbm, tile_bin_hbm, bins_hbm,
    order_hbm, out_ref,
    tiles, weight, azimuth, values, variances, tile_bin, bins, order,
    own_sums, sums, own_obs, every_obs, own_taper, every_taper,
    held, weights, selects, value_cols, root_cols, var_rows, tile_weights, gathered,
    panel, upper, stage, scaled_all, change_all,
    load_sem, sum_send, sum_recv, obs_send, obs_recv, taper_send, taper_recv,
):
    me, layer = lax.axis_index("obs"), lax.axis_index("rows")
    feet = weight.shape[0]
    batches, per = own_obs.shape[0], own_obs.shape[1]
    count, nobs = bins.shape
    tiles_dev, half = tile_bin.shape[0], TILE // 2
    padded = var_rows.shape[0]

    pairs = [
        (order_hbm, order), (value_hbm, values), (var_hbm, variances), (azimuth_hbm, azimuth), (tiles_hbm, tiles),
        (tile_bin_hbm, tile_bin), (state_hbm, out_ref), (weight_hbm, weight), (bins_hbm, bins),
    ]
    loads = [pltpu.make_async_copy(source, target, load_sem.at[i]) for i, (source, target) in enumerate(pairs)]
    for load in loads:
        load.start()
    barrier = pltpu.get_barrier_semaphore()
    for k in range(1, groups):
        pl.semaphore_signal(barrier, inc=1, device_id={"obs": lax.rem(me + k, groups)}, device_id_type=MESH)
    for k in range(1, layers):
        pl.semaphore_signal(barrier, inc=1, device_id={"rows": lax.rem(layer + k, layers)}, device_id_type=MESH)
    for load in loads[:8]:
        load.wait()

    partial = [jnp.zeros((feet, MEMBERS), F32) for _ in range(2)]
    listed = [column_of(tiles[t : t + 1, :].astype(F32)).astype(jnp.int32) for t in range(tiles.shape[0])]
    for tile in range(tiles_dev):
        number = layer * tiles_dev + tile
        chosen = jnp.zeros((feet, TILE), F32)
        for t in range(tiles.shape[0]):
            chosen = chosen + jnp.where(listed[t] == number, weight[:, t, :], 0.0)
        for h in range(2):
            partial[h] = partial[h] + jnp.dot(
                chosen[:, h * half : (h + 1) * half],
                out_ref[pl.ds(tile * TILE + h * half, half), :],
                precision=HIGH,
                preferred_element_type=F32,
            )
    for h in range(2):
        own_sums[h] = partial[h]
    loads[8].wait()
    pl.semaphore_wait(barrier, groups + layers - 2)

    def sum_copy(k):
        return pltpu.make_async_remote_copy(
            own_sums, sums.at[k], sum_send.at[k], sum_recv.at[k],
            device_id={"rows": lax.rem(layer + k, layers)}, device_id_type=MESH,
        )

    def obs_copy(k, b):
        return pltpu.make_async_remote_copy(
            own_obs.at[b], every_obs.at[b, me], obs_send.at[k, b], obs_recv.at[k, b],
            device_id={"obs": lax.rem(me + k, groups)}, device_id_type=MESH,
        )

    def taper_copy(k, b):
        wide = pl.ds(0, b * BATCH)
        return pltpu.make_async_remote_copy(
            own_taper.at[b, :, wide], every_taper.at[b, me, :, wide], taper_send.at[k, b], taper_recv.at[k, b],
            device_id={"obs": lax.rem(me + k, groups)}, device_id_type=MESH,
        )

    def peers(action):
        def one(k, carry):
            action(k)
            return carry

        lax.fori_loop(1, groups, one, 0)

    for k in range(1, layers):
        sum_copy(k).start()

    order_rows = [order[pl.ds(BATCH * q, BATCH)].reshape(1, BATCH) for q in range(batches)]
    base = me * count
    order_wide = jnp.concatenate(order_rows, 1)
    steps = iota((count, nobs), 1).astype(F32)
    member = jnp.logical_and(order_wide >= base, order_wide < base + count).astype(F32)
    local = iota((count, 1), 0)
    at = jnp.sum(jnp.where(order_wide == base + local, steps, 0.0), axis=1, keepdims=True)
    rank = jnp.sum(jnp.where(steps < at, member, 0.0), axis=1, keepdims=True)
    square = (count, count)
    rank_row = jnp.sum(jnp.where(iota(square, 0) == iota(square, 1), rank, 0.0), axis=0, keepdims=True)
    chooser = (iota(square, 0).astype(F32) == rank_row).astype(F32)
    ranked = jnp.dot(
        chooser.astype(BF16), taper_weight(bins[...]).astype(BF16), preferred_element_type=F32
    )
    for n in range(batches - 1):
        rest = count - (n + 1) * per
        index = jnp.broadcast_to(order_rows[n], (rest, BATCH))
        block = lookup([ranked[count - rest :, q * BATCH : (q + 1) * BATCH] for q in range(batches)], index)
        for b in range(n + 1, batches):
            own_taper[b, :, n * BATCH : (n + 1) * BATCH] = block[(b - n - 1) * per : (b - n) * per, :]
    for b in range(1, batches):
        every_taper[b, me, :, : b * BATCH] = own_taper[b, :, : b * BATCH]
    early = min(4, batches)
    for b in range(1, early):
        peers(lambda k: taper_copy(k, b).start())

    foot_of = (iota((count, feet), 0) // (count // feet) == iota((count, feet), 1)).astype(F32)
    spread_feet = jnp.dot(chooser.astype(BF16), foot_of.astype(BF16), preferred_element_type=F32).astype(BF16)
    angles = azimuth[...].reshape(1, count)
    cosines = jnp.sum(chooser * jnp.cos(angles), axis=1, keepdims=True)
    sines = jnp.sum(chooser * jnp.sin(angles), axis=1, keepdims=True)

    blank = [jnp.zeros((padded - batches, BATCH), jnp.int32)] if padded > batches else []
    orders = jnp.concatenate(order_rows + blank, 0)
    value_rows = lookup([values[pl.ds(BATCH * q, BATCH)].reshape(1, BATCH) for q in range(batches)], orders)
    variance_rows = lookup([variances[pl.ds(BATCH * q, BATCH)].reshape(1, BATCH) for q in range(batches)], orders)
    var_rows[...] = variance_rows
    for tile in range(tiles_dev):
        tapers = taper_weight(tile_bin[tile : tile + 1, :])
        tile_weights[tile] = lookup([tapers[:, q * BATCH : (q + 1) * BATCH] for q in range(batches)], orders)
    before = (iota((BATCH, BATCH), 0) < iota((BATCH, BATCH), 1)).astype(F32).astype(BF16)
    places = []
    for b in range(batches):
        group = order_rows[b] // count
        same = (iota((groups, BATCH), 0) == group).astype(F32)
        earlier = jnp.dot(same.astype(BF16), before, preferred_element_type=F32)
        places.append(group.astype(F32) * per + jnp.sum(same * earlier, axis=0, keepdims=True))
    empty = [jnp.zeros((padded - batches, BATCH), F32)] if padded > batches else []
    columns = jnp.transpose(jnp.concatenate(places + empty + [value_rows, jnp.sqrt(variance_rows)], 0))
    for b in range(batches):
        place = columns[:, b : b + 1]
        selects[b] = (place == iota((BATCH, BATCH), 1).astype(F32)).astype(F32).astype(BF16)
        value_cols[b] = columns[:, padded + b : padded + b + 1]
        root_cols[b] = jnp.broadcast_to(columns[:, 2 * padded + b : 2 * padded + b + 1], (BATCH, BATCH))

    for k in range(1, layers):
        sum_copy(k).wait_recv()
    winds = [own_sums[h] for h in range(2)]
    for k in range(1, layers):
        winds = [winds[h] + sums[k, h] for h in range(2)]
    winds = pick(spread_feet, jnp.concatenate(winds, 1))
    observed = model_function(winds[:, :MEMBERS], winds[:, MEMBERS:], cosines, sines)
    for b in range(batches):
        own_obs[b] = observed[b * per : (b + 1) * per, :]
        every_obs[b, me] = observed[b * per : (b + 1) * per, :]
    for b in range(batches):
        if b >= early:
            peers(lambda k: taper_copy(k, b).start())
        peers(lambda k: obs_copy(k, b).start())

    def prepare(b):
        rows = pl.ds(b * BATCH, BATCH)
        peers(lambda k: obs_copy(k, b).wait_recv())
        if b:
            peers(lambda k: taper_copy(k, b).wait_recv())
        if per % SUB == 0:
            obs = every_obs[b].reshape(BATCH, MEMBERS)
            taper = every_taper[b].reshape(BATCH, nobs)
        else:
            for g in range(groups):
                gathered[g * per : (g + 1) * per, :MEMBERS] = every_obs[b, g]
                gathered[g * per : (g + 1) * per, MEMBERS:] = every_taper[b, g]
            obs, taper = gathered[:, :MEMBERS], gathered[:, MEMBERS:]
        select = selects[b]
        held[rows, :] = pick(select, obs)
        if b:
            known = taper[:, : b * BATCH].astype(BF16)
            weights[rows, : b * BATCH] = jnp.dot(select, known, preferred_element_type=F32)

    def update(ref, place, weight, m):
        value = ref[place, :]
        scaled = (scaled_all[m, :, :MEMBERS], scaled_all[m, :, MEMBERS:])
        change = (change_all[m, :, :MEMBERS], change_all[m, :, MEMBERS:])
        product = dot3(halves(value), scaled, NT) * weight
        ref[place, :] = value + dot3(halves(product), change, NN)

    def update_obs(b, m):
        place = pl.ds(pl.multiple_of(b * BATCH, BATCH), BATCH)
        update(held, place, weights[place, pl.ds(pl.multiple_of(m * BATCH, BATCH), BATCH)], m)

    eye = iota((BATCH, BATCH), 0) == iota((BATCH, BATCH), 1)
    prepare(0)

    def batch_step(num, carry):
        rows = pl.ds(pl.multiple_of(num * BATCH, BATCH), BATCH)
        batch_obs = held[rows, :]
        row_mean = jnp.mean(batch_obs, axis=1, keepdims=True)
        perturb = batch_obs - row_mean
        innov = value_cols[num] - row_mean
        split = halves(perturb)
        scaled = halves(perturb * (1.0 / (MEMBERS - 1)))
        panel[:, :BATCH] = dot3(split, scaled, NT) + jnp.where(eye, var_rows[pl.ds(num, 1), :], 0.0)
        panel[:, BATCH:] = eye.astype(F32)
        factor(panel, root_cols.at[num], upper, stage)
        first = panel[:, :BATCH]
        inverses = halves(jnp.concatenate([first, -panel[:, BATCH:]], 1))
        known = halves(jnp.concatenate([jnp.broadcast_to(innov, (BATCH, MEMBERS)), perturb], 0))
        middle = dot3(inverses, known, NN)
        change = dot3(halves(first), halves(middle), TN)
        scaled_all[num] = jnp.concatenate(scaled, 1)
        change_all[num] = jnp.concatenate(halves(change), 1)

        @pl.when(num == 0)
        def _():
            prepare(1)

        @pl.when(num + 1 < batches)
        def _():
            update_obs(num + 1, num)

        for b in range(2, batches):

            @pl.when(num == b - 2)
            def _():
                prepare(b)

        @pl.when(num + 2 < batches)
        def _():
            def pending(m, inner):
                update_obs(num + 2, m)
                return inner

            lax.fori_loop(0, num + 1, pending, 0)

        for tile in range(tiles_dev):
            update(out_ref, pl.ds(tile * TILE, TILE), tile_weights[tile, pl.ds(num, 1), :], num)
        return carry

    lax.fori_loop(0, batches, batch_step, 0)
    for k in range(1, layers):
        sum_copy(k).wait_send()
    for b in range(batches):
        peers(lambda k: obs_copy(k, b).wait_send())
        if b:
            peers(lambda k: taper_copy(k, b).wait_send())


def shards(state, foot_tiles, foot_weight, azimuth, obs_value, obs_var, tile_bin, obs_bin, order):
    groups, layers = lax.axis_size("obs"), lax.axis_size("rows")
    count, nobs = obs_bin.shape
    batches, feet, tiles_dev = nobs // BATCH, foot_tiles.shape[0], tile_bin.shape[0]
    per, padded = count // batches, (nobs // BATCH + SUB - 1) // SUB * SUB
    dma, vmem = pltpu.SemaphoreType.DMA, pltpu.VMEM
    return pl.pallas_call(
        functools.partial(filter_kernel, groups, layers),
        out_shape=jax.ShapeDtypeStruct(state.shape, F32),
        in_specs=[ANY] * 9,
        out_specs=VMEM,
        scratch_shapes=[
            vmem(foot_tiles.shape[::-1], jnp.int32), vmem(foot_weight.shape, F32), vmem((count,), F32),
            vmem((nobs,), F32), vmem((nobs,), F32), vmem(tile_bin.shape, jnp.int32), vmem(obs_bin.shape, jnp.int32),
            vmem((nobs,), jnp.int32),
            vmem((2, feet, MEMBERS), F32), vmem((layers, 2, feet, MEMBERS), F32),
            vmem((batches, per, MEMBERS), F32), vmem((batches, groups, per, MEMBERS), F32),
            vmem((batches, per, nobs), F32), vmem((batches, groups, per, nobs), F32),
            vmem((nobs, MEMBERS), F32), vmem((nobs, nobs), F32), vmem((batches, BATCH, BATCH), BF16),
            vmem((batches, BATCH, 1), F32), vmem((batches, BATCH, BATCH), F32), vmem((padded, BATCH), F32),
            vmem((tiles_dev, padded, BATCH), F32), vmem((BATCH, MEMBERS + nobs), F32),
            vmem((BATCH, 2 * BATCH), F32), vmem((BATCH // 2, BATCH), F32), vmem((STAGES, SUB, SUB, BATCH), F32),
            vmem((batches, BATCH, 2 * MEMBERS), BF16), vmem((batches, BATCH, 2 * MEMBERS), BF16),
            dma((9,)), dma((layers,)), dma((layers,)), dma((groups, batches)), dma((groups, batches)),
            dma((groups, batches)), dma((groups, batches)),
        ],
        compiler_params=pltpu.CompilerParams(
            collective_id=0, has_side_effects=True, vmem_limit_bytes=48 * 1024 * 1024
        ),
    )(state, foot_tiles.T, foot_weight, azimuth, obs_value, obs_var, tile_bin, obs_bin, order)


def solution(mesh):
    return jax.shard_map(
        shards,
        mesh=mesh,
        in_specs=(
            P(("obs", "rows"), None),
            P("obs", None),
            P("obs", None, None),
            P("obs"),
            P(),
            P(),
            P(("obs", "rows"), None),
            P("obs", None),
            P(),
        ),
        out_specs=P(("obs", "rows"), None),
        check_vma=False,
    )
```

time: 71.5 us -> 59.3 us (0.83)
  Pallas kernels: 62.5 us -> 51 us
    pallas_call x2 -> x1, Pallas kernels: 62.5 us -> 51 us  [shards(): pl.pallas_call(functools.partial(filter_kernel, groups, layers), out_shap...]
    unnamed x9 -> x19, local copies, waits for them, and re-layouts: 4.25 us -> 7.59 us
    another operation x3 -> x0, local copies, waits for them, and re-layouts: 1.56 us -> none  [shards(): given = jnp.stack([obs_value, obs_var], axis=1)]
    broadcast_in_dim x2 -> x0, local copies, waits for them, and re-layouts: 1.54 us -> none  [the longest x1 0.85 us: filter_all(): order[:, None]]
    sin x2 -> x0, local copies, waits for them, and re-layouts: 0.78 us -> none  [shards(): jnp.sin(angles)]
where the time goes in v1:
time: 59.3 us; the launch traced here: 58.6 us
  Pallas kernels  51 us (86%)
  local copies, waits for them, and re-layouts  7.59 us (13%)
    pallas_call x1, Pallas kernels, shards(): pl.pallas_call(functools.partial(filter_kernel, groups, layers), out_shap...  51 us
    unnamed x19, local copies, waits for them, and re-layouts  7.59 us

profile of v1, /device:TPU:0, one launch (start us, length us, event | category | flops | bytes accessed | tf_op | source)
XLA Modules:
  0.0 58.6 jit_solution(5589652488203776944)
XLA Ops:
  0.0 0.0 copy-start.8
  0.0 0.7 %copy-done.8 = f32[96]{0:T(128)S(1)} copy-done((f32[96]{0:T(128)S(1)}, f32[96]{0:T(128)}, u32[]{:S(2)}) %copy-start.8) | copy-done | bytes 408
  0.7 0.0 copy-start
  0.7 1.0 %copy-done = s32[96,768]{1,0:T(8,128)S(1)} copy-done((s32[96,768]{1,0:T(8,128)S(1)}, s32[96,768]{1,0:T(8,128)}, u32[]{:S(2)}) %copy-start) | copy-done | bytes 294936
  1.6 0.0 copy-start.1
  1.6 0.9 %copy-done.1 = f32[256,256]{1,0:T(8,128)S(1)} copy-done((f32[256,256]{1,0:T(8,128)S(1)}, f32[256,256]{1,0:T(8,128)}, u32[]{:S(2)}) %copy-start.1) | copy-done | bytes 262168
  2.6 0.0 copy-start.2
  2.6 0.9 %copy-done.2 = f32[24,4,256]{2,1,0:T(4,128)S(1)} copy-done((f32[24,4,256]{2,1,0:T(4,128)S(1)}, f32[24,4,256]{2,1,0:T(4,128)}, u32[]{:S(2)}) %copy-start.2) | copy-done | bytes 98328
  3.5 0.0 copy-start.3
  3.5 0.7 %copy-done.3 = f32[768]{0:T(1024)S(1)} copy-done((f32[768]{0:T(1024)S(1)}, f32[768]{0:T(1024)}, u32[]{:S(2)}) %copy-start.3) | copy-done | bytes 3096
  4.1 0.0 copy-start.4
  4.2 0.7 %copy-done.4 = f32[768]{0:T(1024)S(1)} copy-done((f32[768]{0:T(1024)S(1)}, f32[768]{0:T(1024)}, u32[]{:S(2)}) %copy-start.4) | copy-done | bytes 3096
  4.8 0.0 copy-start.5
  4.8 0.7 %copy-done.5 = s32[768]{0:T(1024)S(1)} copy-done((s32[768]{0:T(1024)S(1)}, s32[768]{0:T(1024)}, u32[]{:S(2)}) %copy-start.5) | copy-done | bytes 3096
  5.5 0.0 copy-start.6
  5.5 0.7 %copy-done.6 = s32[1,768]{1,0:T(1,128)S(1)} copy-done((s32[1,768]{1,0:T(1,128)S(1)}, s32[1,768]{1,0:T(1,128)}, u32[]{:S(2)}) %copy-start.6) | copy-done | bytes 3096
  6.2 0.0 copy-start.7
  6.2 0.7 %copy-done.7 = s32[24,4]{0,1:T(4,128)S(1)} copy-done((s32[24,4]{0,1:T(4,128)S(1)}, s32[24,4]{0,1:T(4,128)}, u32[]{:S(2)}) %copy-start.7) | copy-done | bytes 408
  6.9 51.0 %shard_map.91 = f32[256,256]{1,0:T(8,128)S(1)} custom-call(f32[256,256]{1,0:T(8,128)S(1)} %copy-done.1, s32[4,24]{1,0:T(4,128)S(1)} %bitcast.1, f32[24,4,256]{2,1,0:T(4,128)S(1)} %copy-done.2, f32[96]{0:T(128)S(1)} %copy-done.8, f32[768]{0:T(1024)S(1)} %copy-done.3, f32[768]{0:T(1024)S(1)} %copy-done.4, s32[1,768]{1,0:T(1,128)S(1)} %copy-done.6, ...), custom_call_target="tpu_custom_call" | custom-call | tf_op jit(solution)/shard_map/pallas_call | solution.py:421
  57.9 0.7 %copy.11 = f32[256,256]{1,0:T(8,128)} copy(f32[256,256]{1,0:T(8,128)S(1)} %shard_map.91) | data formatting | bytes 524288
Async XLA Ops:
  0.0 0.7 %copy-start.8 = (f32[96]{0:T(128)S(1)}, f32[96]{0:T(128)}, u32[]{:S(2)}) copy-start(f32[96]{0:T(128)} %azimuth_hbm.1) | copy-start | bytes 1156
  0.7 1.0 %copy-start = (s32[96,768]{1,0:T(8,128)S(1)}, s32[96,768]{1,0:T(8,128)}, u32[]{:S(2)}) copy-start(s32[96,768]{1,0:T(8,128)} %bins_hbm.1) | copy-start | bytes 884740
  1.6 0.9 %copy-start.1 = (f32[256,256]{1,0:T(8,128)S(1)}, f32[256,256]{1,0:T(8,128)}, u32[]{:S(2)}) copy-start(f32[256,256]{1,0:T(8,128)} %state_hbm.1) | copy-start | bytes 786436
  2.6 0.9 %copy-start.2 = (f32[24,4,256]{2,1,0:T(4,128)S(1)}, f32[24,4,256]{2,1,0:T(4,128)}, u32[]{:S(2)}) copy-start(f32[24,4,256]{2,1,0:T(4,128)} %weight_hbm.1) | copy-start | bytes 294916
  3.5 0.7 %copy-start.3 = (f32[768]{0:T(1024)S(1)}, f32[768]{0:T(1024)}, u32[]{:S(2)}) copy-start(f32[768]{0:T(1024)} %value_hbm.1) | copy-start | bytes 9220
  4.1 0.7 %copy-start.4 = (f32[768]{0:T(1024)S(1)}, f32[768]{0:T(1024)}, u32[]{:S(2)}) copy-start(f32[768]{0:T(1024)} %var_hbm.1) | copy-start | bytes 9220
  4.8 0.7 %copy-start.5 = (s32[768]{0:T(1024)S(1)}, s32[768]{0:T(1024)}, u32[]{:S(2)}) copy-start(s32[768]{0:T(1024)} %order_hbm.1) | copy-start | bytes 9220
  5.5 0.7 %copy-start.6 = (s32[1,768]{1,0:T(1,128)S(1)}, s32[1,768]{1,0:T(1,128)}, u32[]{:S(2)}) copy-start(s32[1,768]{1,0:T(1,128)} %tile_bin_hbm.1) | copy-start | bytes 9220
  6.2 0.7 %copy-start.7 = (s32[24,4]{0,1:T(4,128)S(1)}, s32[24,4]{0,1:T(4,128)}, u32[]{:S(2)}) copy-start(s32[24,4]{0,1:T(4,128)} %param.10) | copy-start | bytes 1156

commit v2 on v1

--- a/solution.py
+++ b/solution.py
@@ -439,7 +439,7 @@
             dma((groups, batches)), dma((groups, batches)),
         ],
         compiler_params=pltpu.CompilerParams(
-            collective_id=0, has_side_effects=True, vmem_limit_bytes=48 * 1024 * 1024
+            collective_id=0, has_side_effects=True, vmem_limit_bytes=67043328
         ),
     )(state, foot_tiles.T, foot_weight, azimuth, obs_value, obs_var, tile_bin, obs_bin, order)
 

time: 59.3 us -> 53.3 us (0.90)
  local copies, waits for them, and re-layouts: 7.59 us -> 1.67 us
    unnamed x19 -> x1, local copies, waits for them, and re-layouts: 7.59 us -> 1.67 us
where the time goes in v2:
time: 53.3 us; the launch traced here: 53.1 us
  Pallas kernels  51.4 us (96%)
  local copies, waits for them, and re-layouts  1.67 us (3%)
    pallas_call x1, Pallas kernels, shards(): pl.pallas_call(functools.partial(filter_kernel, groups, layers), out_shap...  51.4 us
    unnamed x1, local copies, waits for them, and re-layouts  1.67 us

profile of v2, /device:TPU:0, one launch (start us, length us, event | category | flops | bytes accessed | tf_op | source)
XLA Modules:
  0.0 53.1 jit_solution(14920949292703882612)
XLA Ops:
  0.0 51.4 %shard_map.91 = f32[256,256]{1,0:T(8,128)} custom-call(f32[256,256]{1,0:T(8,128)} %state_hbm.1, s32[4,24]{1,0:T(4,128)} %bitcast.1, f32[24,4,256]{2,1,0:T(4,128)} %weight_hbm.1, f32[96]{0:T(128)} %azimuth_hbm.1, f32[768]{0:T(1024)} %value_hbm.1, f32[768]{0:T(1024)} %var_hbm.1, s32[1,768]{1,0:T(1,128)} %tile_bin_hbm.1, s32[96,768]{1,0:T(8,128)} %bins_hbm.1, ...), custom_call_target="tpu_custom_call" | custom-call | tf_op jit(solution)/shard_map/pallas_call | solution.py:421
  51.4 1.7 %copy.11 = f32[256,256]{1,0:T(8,128)} copy(f32[256,256]{1,0:T(8,128)} %shard_map.91) | data formatting | bytes 524288

commit v3 on v2

--- a/solution.py
+++ b/solution.py
@@ -13,6 +13,8 @@
 RADIUS = 8
 SUB = 8
 STAGES = 8
+SPAN = 16
+LAGGED = 3
 F32 = jnp.float32
 BF16 = jnp.bfloat16
 
@@ -61,8 +63,8 @@
     return terms[0]
 
 
-def factor(panel, roots, upper, stage):
-    blocks, half = BATCH // SUB, BATCH // 2
+def factor(panel, roots, upper, stage, fill):
+    blocks, group = BATCH // SUB, upper.shape[0] // SUB
     lane = lax.broadcasted_iota(jnp.int32, (SUB, BATCH), 1)
     sub = lax.broadcasted_iota(jnp.int32, (SUB, BATCH), 0)
     left, right = pl.ds(0, BATCH), pl.ds(BATCH, BATCH)
@@ -79,7 +81,8 @@
 
     for b in range(blocks):
         base = SUB * b
-        end = blocks if base >= half else blocks // 2
+        end = (b // group + 1) * group
+        border = SUB * end
         inside = jnp.logical_and(lane >= base, lane < base + SUB)
         start = panel[rows(b), left]
         given = panel[rows(b), right]
@@ -120,8 +123,8 @@
         forward = forward * scale
         lower = jnp.where(lane <= sub + base, forward, 0.0)
         panel[rows(b), left] = lower
-        if base < half:
-            upper[rows(b), :] = jnp.where(lane < half, lower, forward)
+        if end < blocks:
+            upper[rows(b % group), :] = jnp.where(lane < border, lower, forward)
         gain = 1.0 / (diagonal + root)
         own = given
         for k, _, _, _, low, next_low, one, two, below in steps:
@@ -140,13 +143,15 @@
                 panel[rows(i), left] = value - total([columns[k] * down(solved, k) for k in range(SUB)])
                 panel[rows(i), right] = panel[rows(i), right] - total([columns[k] * down(spread, k) for k in range(SUB)])
         elif end < blocks:
-            far = pl.ds(half, half)
+            inner, far = pl.ds(border - SUB * group, SUB * group), pl.ds(border, BATCH - border)
             outer = halves(upper[...])
-            wide = lax.broadcasted_iota(jnp.int32, (half, BATCH), 1)
-            change = dot3(outer, outer, TN)[half:, :]
-            panel[far, left] = jnp.where(wide < half, 0.0, panel[far, left]) - change
-            change = dot3(outer, halves(panel[:half, right]), TN)[half:, :]
+            wide = iota((BATCH - border, BATCH), 1)
+            joined = jnp.logical_and(wide >= border - SUB * group, wide < border)
+            change = dot3(outer, outer, TN)[border:, :]
+            panel[far, left] = jnp.where(joined, 0.0, panel[far, left]) - change
+            change = dot3(outer, halves(panel[inner, right]), TN)[border:, :]
             panel[far, right] = panel[far, right] - change
+        fill(b)
 
 
 def pick(select, value):
@@ -325,11 +330,13 @@
             peers(lambda k: taper_copy(k, b).start())
         peers(lambda k: obs_copy(k, b).start())
 
-    def prepare(b):
-        rows = pl.ds(b * BATCH, BATCH)
+    def arrive(b):
         peers(lambda k: obs_copy(k, b).wait_recv())
         if b:
             peers(lambda k: taper_copy(k, b).wait_recv())
+
+    def prepare(b):
+        rows = pl.ds(b * BATCH, BATCH)
         if per % SUB == 0:
             obs = every_obs[b].reshape(BATCH, MEMBERS)
             taper = every_taper[b].reshape(BATCH, nobs)
@@ -344,66 +351,85 @@
             known = taper[:, : b * BATCH].astype(BF16)
             weights[rows, : b * BATCH] = jnp.dot(select, known, preferred_element_type=F32)
 
-    def update(ref, place, weight, m):
-        value = ref[place, :]
-        scaled = (scaled_all[m, :, :MEMBERS], scaled_all[m, :, MEMBERS:])
-        change = (change_all[m, :, :MEMBERS], change_all[m, :, MEMBERS:])
-        product = dot3(halves(value), scaled, NT) * weight
-        ref[place, :] = value + dot3(halves(product), change, NN)
+    def update(ref, first, weight, m):
+        place = pl.ds(first, BATCH)
+        product = []
+
+        def measure():
+            scaled = (scaled_all[m, :, :MEMBERS], scaled_all[m, :, MEMBERS:])
+            product.append(halves(dot3(halves(ref[place, :]), scaled, NT) * weight()))
+
+        def apply():
+            change = (change_all[m, :, :MEMBERS], change_all[m, :, MEMBERS:])
+            ref[place, :] = ref[place, :] + dot3(product[0], change, NN)
+
+        return [measure, apply]
 
     def update_obs(b, m):
-        place = pl.ds(pl.multiple_of(b * BATCH, BATCH), BATCH)
-        update(held, place, weights[place, pl.ds(pl.multiple_of(m * BATCH, BATCH), BATCH)], m)
+        return update(held, b * BATCH, lambda: weights[pl.ds(b * BATCH, BATCH), pl.ds(m * BATCH, BATCH)], m)
+
+    def update_state(m):
+        work = []
+        for first in range(0, tiles_dev * TILE, BATCH):
+            work += update(out_ref, first, lambda tile=first // TILE: tile_weights[tile, pl.ds(m, 1), :], m)
+        return work
 
     eye = iota((BATCH, BATCH), 0) == iota((BATCH, BATCH), 1)
-    prepare(0)
-
-    def batch_step(num, carry):
-        rows = pl.ds(pl.multiple_of(num * BATCH, BATCH), BATCH)
-        batch_obs = held[rows, :]
+
+    def gains(n, work):
+        batch_obs = held[pl.ds(n * BATCH, BATCH), :]
         row_mean = jnp.mean(batch_obs, axis=1, keepdims=True)
         perturb = batch_obs - row_mean
-        innov = value_cols[num] - row_mean
+        innov = value_cols[n] - row_mean
         split = halves(perturb)
         scaled = halves(perturb * (1.0 / (MEMBERS - 1)))
-        panel[:, :BATCH] = dot3(split, scaled, NT) + jnp.where(eye, var_rows[pl.ds(num, 1), :], 0.0)
+        panel[:, :BATCH] = dot3(split, scaled, NT) + jnp.where(eye, var_rows[pl.ds(n, 1), :], 0.0)
         panel[:, BATCH:] = eye.astype(F32)
-        factor(panel, root_cols.at[num], upper, stage)
+        queue, slots = list(work), BATCH // SUB
+
+        def fill(b):
+            for _ in range(-(-len(queue) // (slots - b))):
+                queue.pop(0)()
+
+        factor(panel, root_cols.at[n], upper, stage, fill)
         first = panel[:, :BATCH]
         inverses = halves(jnp.concatenate([first, -panel[:, BATCH:]], 1))
         known = halves(jnp.concatenate([jnp.broadcast_to(innov, (BATCH, MEMBERS)), perturb], 0))
         middle = dot3(inverses, known, NN)
         change = dot3(halves(first), halves(middle), TN)
-        scaled_all[num] = jnp.concatenate(scaled, 1)
-        change_all[num] = jnp.concatenate(halves(change), 1)
-
-        @pl.when(num == 0)
-        def _():
+        scaled_all[n] = jnp.concatenate(scaled, 1)
+        change_all[n] = jnp.concatenate(halves(change), 1)
+
+    def run(work):
+        for step in work:
+            step()
+
+    applied = [0] * batches
+    arrive(0)
+    prepare(0)
+    for n in range(batches):
+        work = []
+        if n:
+            for b in [2, 3] if n == 1 else [n + 2]:
+                if b < batches:
+                    arrive(b)
+                    work.append(functools.partial(prepare, b))
+        room = LAGGED
+        for b in range(n + 1, min(n + 3, batches)):
+            while applied[b] < n and (b == n + 1 or room > 0):
+                work += update_obs(b, applied[b])
+                applied[b] += 1
+                room -= 1
+        if n:
+            work += update_state(n - 1)
+        gains(n, work)
+        if n == 0 and batches > 1:
+            arrive(1)
             prepare(1)
-
-        @pl.when(num + 1 < batches)
-        def _():
-            update_obs(num + 1, num)
-
-        for b in range(2, batches):
-
-            @pl.when(num == b - 2)
-            def _():
-                prepare(b)
-
-        @pl.when(num + 2 < batches)
-        def _():
-            def pending(m, inner):
-                update_obs(num + 2, m)
-                return inner
-
-            lax.fori_loop(0, num + 1, pending, 0)
-
-        for tile in range(tiles_dev):
-            update(out_ref, pl.ds(tile * TILE, TILE), tile_weights[tile, pl.ds(num, 1), :], num)
-        return carry
-
-    lax.fori_loop(0, batches, batch_step, 0)
+        if n + 1 < batches:
+            run(update_obs(n + 1, n))
+            applied[n + 1] = n + 1
+    run(update_state(batches - 1))
     for k in range(1, layers):
         sum_copy(k).wait_send()
     for b in range(batches):
@@ -433,7 +459,7 @@
             vmem((nobs, MEMBERS), F32), vmem((nobs, nobs), F32), vmem((batches, BATCH, BATCH), BF16),
             vmem((batches, BATCH, 1), F32), vmem((batches, BATCH, BATCH), F32), vmem((padded, BATCH), F32),
             vmem((tiles_dev, padded, BATCH), F32), vmem((BATCH, MEMBERS + nobs), F32),
-            vmem((BATCH, 2 * BATCH), F32), vmem((BATCH // 2, BATCH), F32), vmem((STAGES, SUB, SUB, BATCH), F32),
+            vmem((BATCH, 2 * BATCH), F32), vmem((SPAN, BATCH), F32), vmem((STAGES, SUB, SUB, BATCH), F32),
             vmem((batches, BATCH, 2 * MEMBERS), BF16), vmem((batches, BATCH, 2 * MEMBERS), BF16),
             dma((9,)), dma((layers,)), dma((layers,)), dma((groups, batches)), dma((groups, batches)),
             dma((groups, batches)), dma((groups, batches)),

time: 53.3 us -> 47.2 us (0.89)
  Pallas kernels: 51.4 us -> 45.4 us
    pallas_call x1, Pallas kernels: 51.4 us -> 45.4 us  [shards(): pl.pallas_call(functools.partial(filter_kernel, groups, layers), out_shap...]
where the time goes in v3:
time: 47.2 us; the launch traced here: 47.1 us
  Pallas kernels  45.4 us (96%)
  local copies, waits for them, and re-layouts  1.67 us (4%)
    pallas_call x1, Pallas kernels, shards(): pl.pallas_call(functools.partial(filter_kernel, groups, layers), out_shap...  45.4 us
    unnamed x1, local copies, waits for them, and re-layouts  1.67 us

profile of v3, /device:TPU:0, one launch (start us, length us, event | category | flops | bytes accessed | tf_op | source)
XLA Modules:
  0.0 47.1 jit_solution(421990861679593215)
XLA Ops:
  0.0 45.4 %shard_map.91 = f32[256,256]{1,0:T(8,128)} custom-call(f32[256,256]{1,0:T(8,128)} %state_hbm.1, s32[4,24]{1,0:T(4,128)} %bitcast.1, f32[24,4,256]{2,1,0:T(4,128)} %weight_hbm.1, f32[96]{0:T(128)} %azimuth_hbm.1, f32[768]{0:T(1024)} %value_hbm.1, f32[768]{0:T(1024)} %var_hbm.1, s32[1,768]{1,0:T(1,128)} %tile_bin_hbm.1, s32[96,768]{1,0:T(8,128)} %bins_hbm.1, ...), custom_call_target="tpu_custom_call" | custom-call | tf_op jit(solution)/shard_map/pallas_call | solution.py:447
  45.4 1.7 %copy.11 = f32[256,256]{1,0:T(8,128)} copy(f32[256,256]{1,0:T(8,128)} %shard_map.91) | data formatting | bytes 524288

commit v4 on v3

--- a/solution.py
+++ b/solution.py
@@ -14,7 +14,6 @@
 SUB = 8
 STAGES = 8
 SPAN = 16
-LAGGED = 3
 F32 = jnp.float32
 BF16 = jnp.bfloat16
 
@@ -239,16 +238,33 @@
 
     def obs_copy(k, b):
         return pltpu.make_async_remote_copy(
-            own_obs.at[b], every_obs.at[b, me], obs_send.at[k, b], obs_recv.at[k, b],
+            own_obs.at[b], every_obs.at[b, me], obs_send.at[b], obs_recv.at[b],
             device_id={"obs": lax.rem(me + k, groups)}, device_id_type=MESH,
         )
 
     def taper_copy(k, b):
         wide = pl.ds(0, b * BATCH)
         return pltpu.make_async_remote_copy(
-            own_taper.at[b, :, wide], every_taper.at[b, me, :, wide], taper_send.at[k, b], taper_recv.at[k, b],
+            own_taper.at[b, :, wide], every_taper.at[b, me, :, wide], taper_send.at[b], taper_recv.at[b],
             device_id={"obs": lax.rem(me + k, groups)}, device_id_type=MESH,
         )
+
+    def all_copies(b):
+        others, right = pl.ds(0, groups - 1), {"obs": lax.rem(me + 1, groups)}
+        copies = [
+            pltpu.make_async_remote_copy(
+                every_obs.at[b, others], every_obs.at[b, others], obs_send.at[b], obs_recv.at[b],
+                device_id=right, device_id_type=MESH,
+            )
+        ]
+        if b:
+            part = every_taper.at[b, others, :, pl.ds(0, b * BATCH)]
+            copies.append(
+                pltpu.make_async_remote_copy(
+                    part, part, taper_send.at[b], taper_recv.at[b], device_id=right, device_id_type=MESH,
+                )
+            )
+        return copies
 
     def peers(action):
         def one(k, carry):
@@ -331,9 +347,8 @@
         peers(lambda k: obs_copy(k, b).start())
 
     def arrive(b):
-        peers(lambda k: obs_copy(k, b).wait_recv())
-        if b:
-            peers(lambda k: taper_copy(k, b).wait_recv())
+        for copy in all_copies(b):
+            copy.wait_recv()
 
     def prepare(b):
         rows = pl.ds(b * BATCH, BATCH)
@@ -351,32 +366,51 @@
             known = taper[:, : b * BATCH].astype(BF16)
             weights[rows, : b * BATCH] = jnp.dot(select, known, preferred_element_type=F32)
 
-    def update(ref, first, weight, m):
-        place = pl.ds(first, BATCH)
+    def members_of(place):
+        kind, number = place
+        return (held, number * BATCH, BATCH) if kind == "obs" else (out_ref, number * TILE, TILE)
+
+    def weight_of(place, m):
+        kind, number = place
+        if kind == "obs":
+            return weights[pl.ds(number * BATCH, BATCH), pl.ds(m * BATCH, BATCH)]
+        return jnp.broadcast_to(tile_weights[number, pl.ds(m, 1), :], (TILE, BATCH))
+
+    def load(places):
+        values = []
+        for place in places:
+            ref, first, size = members_of(place)
+            values.append(ref[pl.ds(first, size), :])
+        return jnp.concatenate(values, 0)
+
+    def store(places, value):
+        done = 0
+        for place in places:
+            ref, first, size = members_of(place)
+            ref[pl.ds(first, size), :] = value[done : done + size, :]
+            done += size
+
+    def measure(places, scaled, m):
+        product = dot3(halves(load(places)), scaled, NT)
+        return product * jnp.concatenate([weight_of(place, m) for place in places], 0)
+
+    def lagged(places, m):
         product = []
 
-        def measure():
+        def first():
             scaled = (scaled_all[m, :, :MEMBERS], scaled_all[m, :, MEMBERS:])
-            product.append(halves(dot3(halves(ref[place, :]), scaled, NT) * weight()))
-
-        def apply():
+            product.append(halves(measure(places, scaled, m)))
+
+        def second():
             change = (change_all[m, :, :MEMBERS], change_all[m, :, MEMBERS:])
-            ref[place, :] = ref[place, :] + dot3(product[0], change, NN)
-
-        return [measure, apply]
-
-    def update_obs(b, m):
-        return update(held, b * BATCH, lambda: weights[pl.ds(b * BATCH, BATCH), pl.ds(m * BATCH, BATCH)], m)
-
-    def update_state(m):
-        work = []
-        for first in range(0, tiles_dev * TILE, BATCH):
-            work += update(out_ref, first, lambda tile=first // TILE: tile_weights[tile, pl.ds(m, 1), :], m)
-        return work
+            store(places, load(places) + dot3(product[0], change, NN))
+
+        return [first, second]
 
     eye = iota((BATCH, BATCH), 0) == iota((BATCH, BATCH), 1)
-
-    def gains(n, work):
+    states = [("state", tile) for tile in range(tiles_dev)]
+
+    def gains(n, work, ahead):
         batch_obs = held[pl.ds(n * BATCH, BATCH), :]
         row_mean = jnp.mean(batch_obs, axis=1, keepdims=True)
         perturb = batch_obs - row_mean
@@ -385,7 +419,10 @@
         scaled = halves(perturb * (1.0 / (MEMBERS - 1)))
         panel[:, :BATCH] = dot3(split, scaled, NT) + jnp.where(eye, var_rows[pl.ds(n, 1), :], 0.0)
         panel[:, BATCH:] = eye.astype(F32)
-        queue, slots = list(work), BATCH // SUB
+        scaled_all[n] = jnp.concatenate(scaled, 1)
+        queue, slots, products = list(work), BATCH // SUB, []
+        if ahead and (n or ahead == states):
+            queue.append(lambda: products.append(halves(measure(ahead, scaled, n))))
 
         def fill(b):
             for _ in range(-(-len(queue) // (slots - b))):
@@ -395,47 +432,49 @@
         first = panel[:, :BATCH]
         inverses = halves(jnp.concatenate([first, -panel[:, BATCH:]], 1))
         known = halves(jnp.concatenate([jnp.broadcast_to(innov, (BATCH, MEMBERS)), perturb], 0))
-        middle = dot3(inverses, known, NN)
-        change = dot3(halves(first), halves(middle), TN)
-        scaled_all[n] = jnp.concatenate(scaled, 1)
-        change_all[n] = jnp.concatenate(halves(change), 1)
-
-    def run(work):
-        for step in work:
-            step()
+        middle = halves(dot3(inverses, known, NN))
+        first = halves(first)
+        if n == 0 and ahead != states:
+            arrive(1)
+            prepare(1)
+            products.append(halves(measure(ahead, scaled, n)))
+        rotated = halves(dot3(products[0], first, NT))
+        store(ahead, load(ahead) + dot3(rotated, middle, NN))
+
+        def change():
+            change_all[n] = jnp.concatenate(halves(dot3(first, middle, TN)), 1)
+
+        return change
 
     applied = [0] * batches
     arrive(0)
     prepare(0)
+    change = None
     for n in range(batches):
-        work = []
+        work = [change] if n else []
         if n:
             for b in [2, 3] if n == 1 else [n + 2]:
                 if b < batches:
                     arrive(b)
                     work.append(functools.partial(prepare, b))
-        room = LAGGED
-        for b in range(n + 1, min(n + 3, batches)):
-            while applied[b] < n and (b == n + 1 or room > 0):
-                work += update_obs(b, applied[b])
-                applied[b] += 1
-                room -= 1
-        if n:
-            work += update_state(n - 1)
-        gains(n, work)
-        if n == 0 and batches > 1:
-            arrive(1)
-            prepare(1)
+            seen = [b for b in range(n + 1, min(n + 3, batches))]
+            for m in range(n):
+                places = [("obs", b) for b in seen if applied[b] <= m]
+                if m == n - 1:
+                    places = places + states
+                if places:
+                    work += lagged(places, m)
+            for b in seen:
+                applied[b] = n
+        ahead = [("obs", n + 1)] if n + 1 < batches else states
+        change = gains(n, work, ahead)
         if n + 1 < batches:
-            run(update_obs(n + 1, n))
             applied[n + 1] = n + 1
-    run(update_state(batches - 1))
     for k in range(1, layers):
         sum_copy(k).wait_send()
     for b in range(batches):
-        peers(lambda k: obs_copy(k, b).wait_send())
-        if b:
-            peers(lambda k: taper_copy(k, b).wait_send())
+        for copy in all_copies(b):
+            copy.wait_send()
 
 
 def shards(state, foot_tiles, foot_weight, azimuth, obs_value, obs_var, tile_bin, obs_bin, order):
@@ -461,8 +500,7 @@
             vmem((tiles_dev, padded, BATCH), F32), vmem((BATCH, MEMBERS + nobs), F32),
             vmem((BATCH, 2 * BATCH), F32), vmem((SPAN, BATCH), F32), vmem((STAGES, SUB, SUB, BATCH), F32),
             vmem((batches, BATCH, 2 * MEMBERS), BF16), vmem((batches, BATCH, 2 * MEMBERS), BF16),
-            dma((9,)), dma((layers,)), dma((layers,)), dma((groups, batches)), dma((groups, batches)),
-            dma((groups, batches)), dma((groups, batches)),
+            dma((9,)), dma((layers,)), dma((layers,)), dma((batches,)), dma((batches,)), dma((batches,)), dma((batches,)),
         ],
         compiler_params=pltpu.CompilerParams(
             collective_id=0, has_side_effects=True, vmem_limit_bytes=67043328

time: 47.2 us -> 43.5 us (0.922)
  Pallas kernels: 45.4 us -> 41.6 us
    pallas_call x1, Pallas kernels: 45.4 us -> 41.6 us  [shards(): pl.pallas_call(functools.partial(filter_kernel, groups, layers), out_shap...]
where the time goes in v4:
time: 43.5 us; the launch traced here: 43.3 us
  Pallas kernels  41.6 us (96%)
  local copies, waits for them, and re-layouts  1.67 us (4%)
    pallas_call x1, Pallas kernels, shards(): pl.pallas_call(functools.partial(filter_kernel, groups, layers), out_shap...  41.6 us
    unnamed x1, local copies, waits for them, and re-layouts  1.67 us

profile of v4, /device:TPU:0, one launch (start us, length us, event | category | flops | bytes accessed | tf_op | source)
XLA Modules:
  0.0 43.3 jit_solution(15682187294698998534)
XLA Ops:
  0.0 41.6 %shard_map.91 = f32[256,256]{1,0:T(8,128)} custom-call(f32[256,256]{1,0:T(8,128)} %state_hbm.1, s32[4,24]{1,0:T(4,128)} %bitcast.1, f32[24,4,256]{2,1,0:T(4,128)} %weight_hbm.1, f32[96]{0:T(128)} %azimuth_hbm.1, f32[768]{0:T(1024)} %value_hbm.1, f32[768]{0:T(1024)} %var_hbm.1, s32[1,768]{1,0:T(1,128)} %tile_bin_hbm.1, s32[96,768]{1,0:T(8,128)} %bins_hbm.1, ...), custom_call_target="tpu_custom_call" | custom-call | tf_op jit(solution)/shard_map/pallas_call | solution.py:486
  41.7 1.7 %copy.11 = f32[256,256]{1,0:T(8,128)} copy(f32[256,256]{1,0:T(8,128)} %shard_map.91) | data formatting | bytes 524288

commit v5 on v4

--- a/solution.py
+++ b/solution.py
@@ -201,13 +201,13 @@
         (tile_bin_hbm, tile_bin), (state_hbm, out_ref), (weight_hbm, weight), (bins_hbm, bins),
     ]
     loads = [pltpu.make_async_copy(source, target, load_sem.at[i]) for i, (source, target) in enumerate(pairs)]
-    for load in loads:
-        load.start()
     barrier = pltpu.get_barrier_semaphore()
     for k in range(1, groups):
         pl.semaphore_signal(barrier, inc=1, device_id={"obs": lax.rem(me + k, groups)}, device_id_type=MESH)
     for k in range(1, layers):
         pl.semaphore_signal(barrier, inc=1, device_id={"rows": lax.rem(layer + k, layers)}, device_id_type=MESH)
+    for load in loads:
+        load.start()
     for load in loads[:8]:
         load.wait()
 
@@ -503,9 +503,12 @@
             dma((9,)), dma((layers,)), dma((layers,)), dma((batches,)), dma((batches,)), dma((batches,)), dma((batches,)),
         ],
         compiler_params=pltpu.CompilerParams(
-            collective_id=0, has_side_effects=True, vmem_limit_bytes=67043328
+            collective_id=0, has_side_effects=True, vmem_limit_bytes=48 * 1024 * 1024
         ),
-    )(state, foot_tiles.T, foot_weight, azimuth, obs_value, obs_var, tile_bin, obs_bin, order)
+    )(*(
+        pltpu.with_memory_space_constraint(array, pltpu.MemorySpace.HBM)
+        for array in (state, foot_tiles.T, foot_weight, azimuth, obs_value, obs_var, tile_bin, obs_bin, order)
+    ))
 
 
 def solution(mesh):

time: 43.5 us -> 41.8 us (0.961)
  local copies, waits for them, and re-layouts: 1.67 us -> 0.71 us
  Pallas kernels: 41.6 us -> 40.9 us
    unnamed x1, local copies, waits for them, and re-layouts: 1.67 us -> 0.71 us
    pallas_call x1, Pallas kernels: 41.6 us -> 40.9 us  [shards(): pl.pallas_call(functools.partial(filter_kernel, groups, layers), out_shap...]
where the time goes in v5:
time: 41.8 us; the launch traced here: 41.6 us
  Pallas kernels  40.9 us (98%)
  local copies, waits for them, and re-layouts  0.71 us (2%)
    pallas_call x1, Pallas kernels, shards(): pl.pallas_call(functools.partial(filter_kernel, groups, layers), out_shap...  40.9 us

profile of v5, /device:TPU:0, one launch (start us, length us, event | category | flops | bytes accessed | tf_op | source)
XLA Modules:
  0.0 41.6 jit_solution(6942987281272352008)
XLA Ops:
  0.0 40.9 %shard_map.91 = f32[256,256]{1,0:T(8,128)S(1)} custom-call(f32[256,256]{1,0:T(8,128)} %state_hbm.1, s32[4,24]{1,0:T(4,128)} %bitcast.1, f32[24,4,256]{2,1,0:T(4,128)} %weight_hbm.1, f32[96]{0:T(128)} %azimuth_hbm.1, f32[768]{0:T(1024)} %value_hbm.1, f32[768]{0:T(1024)} %var_hbm.1, s32[1,768]{1,0:T(1,128)} %tile_bin_hbm.1, s32[96,768]{1,0:T(8,128)} %bins_hbm.1, ...), custom_call_target="tpu_custom_call" | custom-call | tf_op jit(solution)/shard_map/pallas_call | solution.py:486
  40.9 0.7 %copy.11 = f32[256,256]{1,0:T(8,128)} copy(f32[256,256]{1,0:T(8,128)S(1)} %shard_map.91) | data formatting | bytes 524288

commit v6 on v5

--- a/solution.py
+++ b/solution.py
@@ -12,8 +12,8 @@
 TILE = 256
 RADIUS = 8
 SUB = 8
-STAGES = 8
 SPAN = 16
+AHEAD = 2
 F32 = jnp.float32
 BF16 = jnp.bfloat16
 
@@ -62,21 +62,23 @@
     return terms[0]
 
 
-def factor(panel, roots, upper, stage, fill):
+def factor(panel, roots, innov_row, solved_innov, upper, fill):
     blocks, group = BATCH // SUB, upper.shape[0] // SUB
     lane = lax.broadcasted_iota(jnp.int32, (SUB, BATCH), 1)
     sub = lax.broadcasted_iota(jnp.int32, (SUB, BATCH), 0)
     left, right = pl.ds(0, BATCH), pl.ds(BATCH, BATCH)
 
-    def across(value, column):
-        lanes = jnp.full((SUB, BATCH), column, jnp.int32)
-        return jnp.take_along_axis(value, lanes, axis=1, mode="promise_in_bounds")
-
     def down(value, row):
         return jnp.broadcast_to(value[row : row + 1, :], (SUB, BATCH))
 
     def rows(i):
         return pl.ds(SUB * i, SUB)
+
+    def column_block(value, i):
+        lanes = sub + SUB * i
+        return [
+            jnp.take_along_axis(down(value, k), lanes, axis=1, mode="promise_in_bounds") for k in range(SUB)
+        ]
 
     for b in range(blocks):
         base = SUB * b
@@ -86,11 +88,9 @@
         start = panel[rows(b), left]
         given = panel[rows(b), right]
         root = roots[rows(b), :]
-        cols = [across(start, base + k) for k in range(SUB)]
-        for i in range(b + 1, end):
-            value = panel[rows(i), left]
-            for k in range(SUB):
-                stage[i % STAGES, k] = across(value, base + k)
+        cols = column_block(start, b)
+        near = min(end + AHEAD, blocks)
+        coefficients = [column_block(start, i) for i in range(b + 1, near)]
         solved = jnp.where(inside, (lane == sub + base).astype(F32), start)
         forward, scale, diagonal, steps = solved, None, None, []
         for k in range(0, SUB, 2):
@@ -122,6 +122,7 @@
         forward = forward * scale
         lower = jnp.where(lane <= sub + base, forward, 0.0)
         panel[rows(b), left] = lower
+        solved_innov[rows(b), :] = jnp.sum(lower * innov_row, axis=1, keepdims=True)
         if end < blocks:
             upper[rows(b % group), :] = jnp.where(lane < border, lower, forward)
         gain = 1.0 / (diagonal + root)
@@ -132,32 +133,34 @@
             rest = own - (low * first + next_low * second)
             own = jnp.where(below, rest, jnp.where(one, first, jnp.where(two, second, own)))
         panel[rows(b), right] = own
-        if b + 1 < end:
+        if b + 1 < near:
             spread = given - root * own
             for k, full_p, full_q, pair, *_ in steps:
                 spread = jnp.where(pair, 0.0, spread) - (full_p * down(spread, k) + full_q * down(spread, k + 1))
-            for i in range(b + 1, end):
-                columns = [stage[i % STAGES, k] for k in range(SUB)]
+            for i, columns in zip(range(b + 1, near), coefficients):
                 value = jnp.where(inside, 0.0, panel[rows(i), left])
                 panel[rows(i), left] = value - total([columns[k] * down(solved, k) for k in range(SUB)])
                 panel[rows(i), right] = panel[rows(i), right] - total([columns[k] * down(spread, k) for k in range(SUB)])
-        elif end < blocks:
-            inner, far = pl.ds(border - SUB * group, SUB * group), pl.ds(border, BATCH - border)
+        if b + 1 == end and near < blocks:
+            inner, first = pl.ds(border - SUB * group, SUB * group), SUB * near
+            far = pl.ds(first, BATCH - first)
             outer = halves(upper[...])
-            wide = iota((BATCH - border, BATCH), 1)
+            wide = iota((BATCH - first, BATCH), 1)
             joined = jnp.logical_and(wide >= border - SUB * group, wide < border)
-            change = dot3(outer, outer, TN)[border:, :]
+            change = dot3(outer, outer, TN)[first:, :]
             panel[far, left] = jnp.where(joined, 0.0, panel[far, left]) - change
-            change = dot3(outer, halves(panel[inner, right]), TN)[border:, :]
+            change = dot3(outer, halves(panel[inner, right]), TN)[first:, :]
             panel[far, right] = panel[far, right] - change
+
         fill(b)
 
 
 def pick(select, value):
     high, rest = halves(value)
     low = (value - high.astype(F32) - rest.astype(F32)).astype(BF16)
-    dot = functools.partial(jnp.dot, preferred_element_type=F32)
-    return dot(select, high) + (dot(select, rest) + dot(select, low))
+    return jnp.dot(
+        jnp.concatenate([select] * 3, 1), jnp.concatenate([high, rest, low], 0), preferred_element_type=F32
+    )
 
 
 def lookup(pieces, index):
@@ -186,7 +189,7 @@
     tiles, weight, azimuth, values, variances, tile_bin, bins, order,
     own_sums, sums, own_obs, every_obs, own_taper, every_taper,
     held, weights, selects, value_cols, root_cols, var_rows, tile_weights, gathered,
-    panel, upper, stage, scaled_all, change_all,
+    panel, solved_innov, upper, scaled_all, change_all,
     load_sem, sum_send, sum_recv, obs_send, obs_recv, taper_send, taper_recv,
 ):
     me, layer = lax.axis_index("obs"), lax.axis_index("rows")
@@ -415,6 +418,7 @@
         row_mean = jnp.mean(batch_obs, axis=1, keepdims=True)
         perturb = batch_obs - row_mean
         innov = value_cols[n] - row_mean
+        innov_row = jnp.sum(jnp.where(eye, innov, 0.0), axis=0, keepdims=True)
         split = halves(perturb)
         scaled = halves(perturb * (1.0 / (MEMBERS - 1)))
         panel[:, :BATCH] = dot3(split, scaled, NT) + jnp.where(eye, var_rows[pl.ds(n, 1), :], 0.0)
@@ -425,14 +429,14 @@
             queue.append(lambda: products.append(halves(measure(ahead, scaled, n))))
 
         def fill(b):
-            for _ in range(-(-len(queue) // (slots - b))):
-                queue.pop(0)()
-
-        factor(panel, root_cols.at[n], upper, stage, fill)
+            left = (slots - b) // 2
+            if b % 2 and left:
+                for _ in range(-(-len(queue) // left)):
+                    queue.pop(0)()
+
+        factor(panel, root_cols.at[n], innov_row, solved_innov, upper, fill)
         first = panel[:, :BATCH]
-        inverses = halves(jnp.concatenate([first, -panel[:, BATCH:]], 1))
-        known = halves(jnp.concatenate([jnp.broadcast_to(innov, (BATCH, MEMBERS)), perturb], 0))
-        middle = halves(dot3(inverses, known, NN))
+        middle = halves(solved_innov[...] - dot3(halves(panel[:, BATCH:]), split, NN))
         first = halves(first)
         if n == 0 and ahead != states:
             arrive(1)
@@ -462,8 +466,8 @@
                 places = [("obs", b) for b in seen if applied[b] <= m]
                 if m == n - 1:
                     places = places + states
-                if places:
-                    work += lagged(places, m)
+                for part in range(0, len(places), 2):
+                    work += lagged(places[part : part + 2], m)
             for b in seen:
                 applied[b] = n
         ahead = [("obs", n + 1)] if n + 1 < batches else states
@@ -498,7 +502,7 @@
             vmem((nobs, MEMBERS), F32), vmem((nobs, nobs), F32), vmem((batches, BATCH, BATCH), BF16),
             vmem((batches, BATCH, 1), F32), vmem((batches, BATCH, BATCH), F32), vmem((padded, BATCH), F32),
             vmem((tiles_dev, padded, BATCH), F32), vmem((BATCH, MEMBERS + nobs), F32),
-            vmem((BATCH, 2 * BATCH), F32), vmem((SPAN, BATCH), F32), vmem((STAGES, SUB, SUB, BATCH), F32),
+            vmem((BATCH, 2 * BATCH), F32), vmem((BATCH, 1), F32), vmem((SPAN, BATCH), F32),
             vmem((batches, BATCH, 2 * MEMBERS), BF16), vmem((batches, BATCH, 2 * MEMBERS), BF16),
             dma((9,)), dma((layers,)), dma((layers,)), dma((batches,)), dma((batches,)), dma((batches,)), dma((batches,)),
         ],

time: 41.8 us -> 37.6 us (0.90)
  Pallas kernels: 40.9 us -> 36.8 us
    pallas_call x1, Pallas kernels: 40.9 us -> 36.8 us  [shards(): pl.pallas_call(functools.partial(filter_kernel, groups, layers), out_shap...]
where the time goes in v6:
time: 37.6 us; the launch traced here: 37.5 us
  Pallas kernels  36.8 us (98%)
  local copies, waits for them, and re-layouts  0.71 us (2%)
    pallas_call x1, Pallas kernels, shards(): pl.pallas_call(functools.partial(filter_kernel, groups, layers), out_shap...  36.8 us

profile of v6, /device:TPU:0, one launch (start us, length us, event | category | flops | bytes accessed | tf_op | source)
XLA Modules:
  0.0 37.5 jit_solution(10002949088309282645)
XLA Ops:
  0.0 36.8 %shard_map.91 = f32[256,256]{1,0:T(8,128)S(1)} custom-call(f32[256,256]{1,0:T(8,128)} %state_hbm.1, s32[4,24]{1,0:T(4,128)} %bitcast.1, f32[24,4,256]{2,1,0:T(4,128)} %weight_hbm.1, f32[96]{0:T(128)} %azimuth_hbm.1, f32[768]{0:T(1024)} %value_hbm.1, f32[768]{0:T(1024)} %var_hbm.1, s32[1,768]{1,0:T(1,128)} %tile_bin_hbm.1, s32[96,768]{1,0:T(8,128)} %bins_hbm.1, ...), custom_call_target="tpu_custom_call" | custom-call | tf_op jit(solution)/shard_map/pallas_call | solution.py:490
  36.8 0.7 %copy.11 = f32[256,256]{1,0:T(8,128)} copy(f32[256,256]{1,0:T(8,128)S(1)} %shard_map.91) | data formatting | bytes 524288

commit v7 on v6

--- a/solution.py
+++ b/solution.py
@@ -190,7 +190,7 @@
     own_sums, sums, own_obs, every_obs, own_taper, every_taper,
     held, weights, selects, value_cols, root_cols, var_rows, tile_weights, gathered,
     panel, solved_innov, upper, scaled_all, change_all,
-    load_sem, sum_send, sum_recv, obs_send, obs_recv, taper_send, taper_recv,
+    load_sem, sum_send, sum_recv, obs_send, obs_recv, taper_send, taper_recv, pass_send, pass_recv,
 ):
     me, layer = lax.axis_index("obs"), lax.axis_index("rows")
     feet = weight.shape[0]
@@ -245,36 +245,45 @@
             device_id={"obs": lax.rem(me + k, groups)}, device_id_type=MESH,
         )
 
+    partner = {"obs": me + 1 - 2 * (me % 2)}
+
+    def taper_part(b, first, size):
+        return every_taper.at[b, pl.ds(first, size), :, pl.ds(0, b * BATCH)]
+
     def taper_copy(k, b):
         wide = pl.ds(0, b * BATCH)
         return pltpu.make_async_remote_copy(
             own_taper.at[b, :, wide], every_taper.at[b, me, :, wide], taper_send.at[b], taper_recv.at[b],
-            device_id={"obs": lax.rem(me + k, groups)}, device_id_type=MESH,
+            device_id={"obs": lax.rem(me + 2 * k, groups)} if k is not None else partner, device_id_type=MESH,
         )
 
-    def all_copies(b):
-        others, right = pl.ds(0, groups - 1), {"obs": lax.rem(me + 1, groups)}
-        copies = [
-            pltpu.make_async_remote_copy(
-                every_obs.at[b, others], every_obs.at[b, others], obs_send.at[b], obs_recv.at[b],
-                device_id=right, device_id_type=MESH,
+    def pass_copy(k, b):
+        part = taper_part(b, lax.rem(me + 2 * k, groups), 1)
+        return pltpu.make_async_remote_copy(
+            part, part, pass_send.at[b], pass_recv.at[b], device_id=partner, device_id_type=MESH,
+        )
+
+    def taper_copies(b):
+        direct, passed = taper_part(b, 0, groups // 2), taper_part(b, 0, groups // 2 - 1)
+        return [
+            pltpu.make_async_remote_copy(part, part, send, recv, device_id=partner, device_id_type=MESH)
+            for part, send, recv in (
+                (direct, taper_send.at[b], taper_recv.at[b]), (passed, pass_send.at[b], pass_recv.at[b])
             )
         ]
-        if b:
-            part = every_taper.at[b, others, :, pl.ds(0, b * BATCH)]
-            copies.append(
-                pltpu.make_async_remote_copy(
-                    part, part, taper_send.at[b], taper_recv.at[b], device_id=right, device_id_type=MESH,
-                )
-            )
-        return copies
-
-    def peers(action):
+
+    def all_obs(b):
+        part = every_obs.at[b, pl.ds(0, groups - 1)]
+        return pltpu.make_async_remote_copy(
+            part, part, obs_send.at[b], obs_recv.at[b], device_id=partner, device_id_type=MESH,
+        )
+
+    def peers(action, last=groups):
         def one(k, carry):
             action(k)
             return carry
 
-        lax.fori_loop(1, groups, one, 0)
+        lax.fori_loop(1, last, one, 0)
 
     for k in range(1, layers):
         sum_copy(k).start()
@@ -301,9 +310,9 @@
             own_taper[b, :, n * BATCH : (n + 1) * BATCH] = block[(b - n - 1) * per : (b - n) * per, :]
     for b in range(1, batches):
         every_taper[b, me, :, : b * BATCH] = own_taper[b, :, : b * BATCH]
-    early = min(4, batches)
-    for b in range(1, early):
-        peers(lambda k: taper_copy(k, b).start())
+    for b in range(1, batches):
+        taper_copy(None, b).start()
+        peers(lambda k: taper_copy(k, b).start(), groups // 2)
 
     foot_of = (iota((count, feet), 0) // (count // feet) == iota((count, feet), 1)).astype(F32)
     spread_feet = jnp.dot(chooser.astype(BF16), foot_of.astype(BF16), preferred_element_type=F32).astype(BF16)
@@ -345,13 +354,15 @@
         own_obs[b] = observed[b * per : (b + 1) * per, :]
         every_obs[b, me] = observed[b * per : (b + 1) * per, :]
     for b in range(batches):
-        if b >= early:
-            peers(lambda k: taper_copy(k, b).start())
         peers(lambda k: obs_copy(k, b).start())
+    for b in range(1, batches):
+        taper_copies(b)[0].wait_recv()
+        peers(lambda k: pass_copy(k, b).start(), groups // 2)
 
     def arrive(b):
-        for copy in all_copies(b):
-            copy.wait_recv()
+        all_obs(b).wait_recv()
+        if b:
+            taper_copies(b)[1].wait_recv()
 
     def prepare(b):
         rows = pl.ds(b * BATCH, BATCH)
@@ -425,8 +436,7 @@
         panel[:, BATCH:] = eye.astype(F32)
         scaled_all[n] = jnp.concatenate(scaled, 1)
         queue, slots, products = list(work), BATCH // SUB, []
-        if ahead and (n or ahead == states):
-            queue.append(lambda: products.append(halves(measure(ahead, scaled, n))))
+        queue.append(lambda: products.append(halves(measure(ahead, scaled, n))))
 
         def fill(b):
             left = (slots - b) // 2
@@ -438,10 +448,6 @@
         first = panel[:, :BATCH]
         middle = halves(solved_innov[...] - dot3(halves(panel[:, BATCH:]), split, NN))
         first = halves(first)
-        if n == 0 and ahead != states:
-            arrive(1)
-            prepare(1)
-            products.append(halves(measure(ahead, scaled, n)))
         rotated = halves(dot3(products[0], first, NT))
         store(ahead, load(ahead) + dot3(rotated, middle, NN))
 
@@ -456,6 +462,8 @@
     change = None
     for n in range(batches):
         work = [change] if n else []
+        if n == 0 and batches > 1:
+            work = [lambda: None] * 3 + [functools.partial(arrive, 1), functools.partial(prepare, 1)]
         if n:
             for b in [2, 3] if n == 1 else [n + 2]:
                 if b < batches:
@@ -477,8 +485,10 @@
     for k in range(1, layers):
         sum_copy(k).wait_send()
     for b in range(batches):
-        for copy in all_copies(b):
-            copy.wait_send()
+        all_obs(b).wait_send()
+        if b:
+            for copy in taper_copies(b):
+                copy.wait_send()
 
 
 def shards(state, foot_tiles, foot_weight, azimuth, obs_value, obs_var, tile_bin, obs_bin, order):
@@ -504,7 +514,7 @@
             vmem((tiles_dev, padded, BATCH), F32), vmem((BATCH, MEMBERS + nobs), F32),
             vmem((BATCH, 2 * BATCH), F32), vmem((BATCH, 1), F32), vmem((SPAN, BATCH), F32),
             vmem((batches, BATCH, 2 * MEMBERS), BF16), vmem((batches, BATCH, 2 * MEMBERS), BF16),
-            dma((9,)), dma((layers,)), dma((layers,)), dma((batches,)), dma((batches,)), dma((batches,)), dma((batches,)),
+            dma((9,)), dma((layers,)), dma((layers,)), *[dma((batches,)) for _ in range(6)],
         ],
         compiler_params=pltpu.CompilerParams(
             collective_id=0, has_side_effects=True, vmem_limit_bytes=48 * 1024 * 1024

time: 37.6 us -> 36.4 us (0.968)
  Pallas kernels: 36.8 us -> 35.5 us
    pallas_call x1, Pallas kernels: 36.8 us -> 35.5 us  [shards(): pl.pallas_call(functools.partial(filter_kernel, groups, layers), out_shap...]
where the time goes in v7:
time: 36.4 us; the launch traced here: 36.2 us
  Pallas kernels  35.5 us (98%)
  local copies, waits for them, and re-layouts  0.71 us (2%)
    pallas_call x1, Pallas kernels, shards(): pl.pallas_call(functools.partial(filter_kernel, groups, layers), out_shap...  35.5 us

profile of v7, /device:TPU:0, one launch (start us, length us, event | category | flops | bytes accessed | tf_op | source)
XLA Modules:
  0.0 36.2 jit_solution(11240303796628065555)
XLA Ops:
  0.0 35.5 %shard_map.91 = f32[256,256]{1,0:T(8,128)S(1)} custom-call(f32[256,256]{1,0:T(8,128)} %state_hbm.1, s32[4,24]{1,0:T(4,128)} %bitcast.1, f32[24,4,256]{2,1,0:T(4,128)} %weight_hbm.1, f32[96]{0:T(128)} %azimuth_hbm.1, f32[768]{0:T(1024)} %value_hbm.1, f32[768]{0:T(1024)} %var_hbm.1, s32[1,768]{1,0:T(1,128)} %tile_bin_hbm.1, s32[96,768]{1,0:T(8,128)} %bins_hbm.1, ...), custom_call_target="tpu_custom_call" | custom-call | tf_op jit(solution)/shard_map/pallas_call | solution.py:500
  35.5 0.7 %copy.11 = f32[256,256]{1,0:T(8,128)} copy(f32[256,256]{1,0:T(8,128)S(1)} %shard_map.91) | data formatting | bytes 524288

commit v8 on v7

--- a/solution.py
+++ b/solution.py
@@ -235,13 +235,13 @@
 
     def sum_copy(k):
         return pltpu.make_async_remote_copy(
-            own_sums, sums.at[k], sum_send.at[k], sum_recv.at[k],
+            own_sums, sums.at[k], sum_send.at[0], sum_recv.at[0],
             device_id={"rows": lax.rem(layer + k, layers)}, device_id_type=MESH,
         )
 
     def obs_copy(k, b):
         return pltpu.make_async_remote_copy(
-            own_obs.at[b], every_obs.at[b, me], obs_send.at[b], obs_recv.at[b],
+            own_obs.at[b], every_obs.at[b, me], obs_send.at[0], obs_recv.at[b],
             device_id={"obs": lax.rem(me + k, groups)}, device_id_type=MESH,
         )
 
@@ -253,14 +253,14 @@
     def taper_copy(k, b):
         wide = pl.ds(0, b * BATCH)
         return pltpu.make_async_remote_copy(
-            own_taper.at[b, :, wide], every_taper.at[b, me, :, wide], taper_send.at[b], taper_recv.at[b],
+            own_taper.at[b, :, wide], every_taper.at[b, me, :, wide], taper_send.at[0], taper_recv.at[b - 1],
             device_id={"obs": lax.rem(me + 2 * k, groups)} if k is not None else partner, device_id_type=MESH,
         )
 
     def pass_copy(k, b):
         part = taper_part(b, lax.rem(me + 2 * k, groups), 1)
         return pltpu.make_async_remote_copy(
-            part, part, pass_send.at[b], pass_recv.at[b], device_id=partner, device_id_type=MESH,
+            part, part, pass_send.at[0], pass_recv.at[b - 1], device_id=partner, device_id_type=MESH,
         )
 
     def taper_copies(b):
@@ -268,14 +268,14 @@
         return [
             pltpu.make_async_remote_copy(part, part, send, recv, device_id=partner, device_id_type=MESH)
             for part, send, recv in (
-                (direct, taper_send.at[b], taper_recv.at[b]), (passed, pass_send.at[b], pass_recv.at[b])
+                (direct, taper_send.at[0], taper_recv.at[b - 1]), (passed, pass_send.at[0], pass_recv.at[b - 1])
             )
         ]
 
     def all_obs(b):
         part = every_obs.at[b, pl.ds(0, groups - 1)]
         return pltpu.make_async_remote_copy(
-            part, part, obs_send.at[b], obs_recv.at[b], device_id=partner, device_id_type=MESH,
+            part, part, obs_send.at[0], obs_recv.at[b], device_id=partner, device_id_type=MESH,
         )
 
     def peers(action, last=groups):
@@ -343,8 +343,12 @@
         value_cols[b] = columns[:, padded + b : padded + b + 1]
         root_cols[b] = jnp.broadcast_to(columns[:, 2 * padded + b : 2 * padded + b + 1], (BATCH, BATCH))
 
-    for k in range(1, layers):
-        sum_copy(k).wait_recv()
+    part = sums.at[pl.ds(0, layers - 1)]
+    all_sums = pltpu.make_async_remote_copy(
+        part, part, sum_send.at[0], sum_recv.at[0],
+        device_id={"rows": lax.rem(layer + 1, layers)}, device_id_type=MESH,
+    )
+    all_sums.wait_recv()
     winds = [own_sums[h] for h in range(2)]
     for k in range(1, layers):
         winds = [winds[h] + sums[k, h] for h in range(2)]
@@ -482,13 +486,15 @@
         change = gains(n, work, ahead)
         if n + 1 < batches:
             applied[n + 1] = n + 1
-    for k in range(1, layers):
-        sum_copy(k).wait_send()
-    for b in range(batches):
-        all_obs(b).wait_send()
-        if b:
-            for copy in taper_copies(b):
-                copy.wait_send()
+    all_sums.wait_send()
+    rows, wide = (batches - 1, batches) if batches % 2 == 0 else (batches, batches - 1)
+    sent = [(every_obs.at[:, pl.ds(0, groups - 1)], obs_send)]
+    for count, semaphore in ((groups // 2, taper_send), (groups // 2 - 1, pass_send)):
+        sent.append((every_taper.at[pl.ds(0, rows), pl.ds(0, count), :, pl.ds(0, wide * BATCH // 2)], semaphore))
+    for part, semaphore in sent:
+        pltpu.make_async_remote_copy(
+            part, part, semaphore.at[0], semaphore.at[0], device_id=partner, device_id_type=MESH
+        ).wait_send()
 
 
 def shards(state, foot_tiles, foot_weight, azimuth, obs_value, obs_var, tile_bin, obs_bin, order):
@@ -514,7 +520,7 @@
             vmem((tiles_dev, padded, BATCH), F32), vmem((BATCH, MEMBERS + nobs), F32),
             vmem((BATCH, 2 * BATCH), F32), vmem((BATCH, 1), F32), vmem((SPAN, BATCH), F32),
             vmem((batches, BATCH, 2 * MEMBERS), BF16), vmem((batches, BATCH, 2 * MEMBERS), BF16),
-            dma((9,)), dma((layers,)), dma((layers,)), *[dma((batches,)) for _ in range(6)],
+            dma((9,)), dma((1,)), dma((1,)), dma((1,)), dma((batches,)), dma((1,)), dma((batches - 1,)), dma((1,)), dma((batches - 1,)),
         ],
         compiler_params=pltpu.CompilerParams(
             collective_id=0, has_side_effects=True, vmem_limit_bytes=48 * 1024 * 1024

time: 36.4 us -> 36.2 us (level)
  no operation moved by 1% of the time
where the time goes in v8:
time: 36.2 us; the launch traced here: 36 us
  Pallas kernels  35.3 us (98%)
  local copies, waits for them, and re-layouts  0.71 us (2%)
    pallas_call x1, Pallas kernels, shards(): pl.pallas_call(functools.partial(filter_kernel, groups, layers), out_shap...  35.3 us

profile of v8, /device:TPU:0, one launch (start us, length us, event | category | flops | bytes accessed | tf_op | source)
XLA Modules:
  0.0 36.0 jit_solution(11798402071828394671)
XLA Ops:
  0.0 35.3 %shard_map.91 = f32[256,256]{1,0:T(8,128)S(1)} custom-call(f32[256,256]{1,0:T(8,128)} %state_hbm.1, s32[4,24]{1,0:T(4,128)} %bitcast.1, f32[24,4,256]{2,1,0:T(4,128)} %weight_hbm.1, f32[96]{0:T(128)} %azimuth_hbm.1, f32[768]{0:T(1024)} %value_hbm.1, f32[768]{0:T(1024)} %var_hbm.1, s32[1,768]{1,0:T(1,128)} %tile_bin_hbm.1, s32[96,768]{1,0:T(8,128)} %bins_hbm.1, ...), custom_call_target="tpu_custom_call" | custom-call | tf_op jit(solution)/shard_map/pallas_call | solution.py:506
  35.3 0.7 %copy.11 = f32[256,256]{1,0:T(8,128)} copy(f32[256,256]{1,0:T(8,128)S(1)} %shard_map.91) | data formatting | bytes 524288
